TPU v7x, 256 devices: a whole 4x4x8 slice. The times are simulated.
256 devices in a mesh: client: 128 (over y, z, x), param: 2 (over core).
Axes of the slice: x: 4, y: 4, z: 8, core: 2. Of those that a mesh axis runs over, the one named last changes fastest.
Arguments:
- updates: float32 [256, 128, 3584], P('client', None, 'param'), as said below
- sample_counts: int32 [256], P('client'), may hold values from 16 to 1023
Outputs:
- median: float32 [128, 3584], P('client', 'param')
- shares: float32 [256], P('client')
Inputs may be any that keep to these rules, and one draw needn't show every extreme that they name: `updates`: each client's update is real-valued with every entry nonzero in general.
All inputs are finite; a program needn't handle non-finite values.
Results may differ from a plain program's by a relative error of at most 0.0001.
Values sent between devices are 32-bit elements; how exact they have to be, the bound alone decides.
No kernel may reach another device: no remote copies, remote signals or barrier semaphores. Data moves between devices by JAX's collectives and lax.ppermute only.
A program may use at most 64 MiB of HBM per device.

v0:
```python
import functools

import jax
import jax.numpy as jnp
from jax import lax
from jax.sharding import Mesh
from jax.sharding import PartitionSpec as P

ITERS = 2
CLIENT = ("client_0", "client_1", "client_2")
CLIENT_PARAM = ("client_0", "client_1", "client_2", "param")


smoothing = 1e-06


def by_axis(shard, axes):
    return functools.reduce(lax.psum, axes, shard)


def weighted_sum(weights, updates):
    return jnp.einsum("c,crk->rk", weights, updates, precision=lax.Precision.HIGHEST)


def local(updates, sample_counts):
    local_clients = updates.shape[0]
    clients = local_clients * lax.axis_size(CLIENT)
    exchanged = lax.all_to_all(updates, CLIENT, split_axis=1, concat_axis=0, tiled=True)
    counts_f = lax.all_gather(sample_counts, CLIENT, axis=0, tiled=True).astype(jnp.float32)
    weights = counts_f
    for iteration in range(ITERS + 1):
        weight_sum = jnp.sum(weights)
        median = weighted_sum(weights, exchanged) / weight_sum
        if iteration < ITERS:
            distance_sq = jnp.sum((exchanged - median[None]) ** 2, axis=(1, 2))
            distance_sq = by_axis(distance_sq, CLIENT_PARAM)
            weights = counts_f / jnp.sqrt(distance_sq + smoothing)
    offset = lax.axis_index(CLIENT) * local_clients
    shares = lax.dynamic_slice_in_dim(clients * weights / weight_sum, offset, local_clients, 0)
    return (median, shares)


def solution(mesh):
    finer = Mesh(
        mesh.devices.reshape(4, 8, 4, mesh.shape["param"]),
        ("client_0", "client_1", "client_2", "param"),
    )
    in_specs = (P(CLIENT, None, "param"), P(CLIENT))
    out_specs = (P(CLIENT, "param"), P(CLIENT))
    return jax.shard_map(local, mesh=finer, in_specs=in_specs, out_specs=out_specs, check_vma=False)
```

profile of v0, /device:TPU:1, one launch (start us, length us, event | category | flops | bytes accessed | tf_op | source)
XLA Modules:
  0.0 168.9 jit_solution(10657067493912830031)
XLA Ops:
  0.6 4.2 %copy.10 = f32[2,128,1792]{2,0,1:T(2,128)} copy(f32[2,128,1792]{2,1,0:T(8,128)} %param.2) | data formatting | bytes 3670016 | tf_op args[0]
  4.8 0.0 copy-start.1
  4.8 0.0 copy-start
  4.8 16.5 %all-to-all-start = ((f32[2,128,1792]{2,0,1:T(2,128)}), f32[2,128,1792]{2,0,1:T(2,128)S(1)}, u32[]{:S(2)}, u32[]{:S(2)}) async-start(f32[2,128,1792]{2,0,1:T(2,128)} %copy.10), calls=%async_computation | async-start | bytes 3670016 | tf_op jit(solution)/shard_map/all_to_all | solution.py:28
  21.3 0.0 copy-done.1
  21.3 0.6 dynamic-slice
  22.5 0.0 copy-done
  22.5 0.2 dynamic-update-slice
  22.8 50.8 %all-reduce = s32[256]{0:T(256)S(1)} all-reduce(s32[256]{0:T(256)S(1)} %dynamic-update-slice), channel_id=1, replica_groups=mesh['client_0'=4,'client_1'=8,'client_2'=4,'param'=2] {'client_0','clie..., use_global_device_ids=true, to_apply=%add | all-reduce | flops 256 | bytes 2048
  73.6 0.6 convert_reduce_fusion
  74.2 0.0 all-to-all-done
  74.2 0.1 copy.22
  74.4 2.7 %copy.12 = f32[128,2,1,1792]{3,1,0,2:T(2,128)} copy(f32[128,2,1,1792]{3,0,2,1:T(8,128)S(1)} %bitcast.25) | data formatting | bytes 3670016 | tf_op jit(solution)/shard_map/all_to_all | solution.py:28
  77.0 3.4 %reshape.48 = f32[256,1792]{1,0:T(8,128)} reshape(f32[128,2,1,1792]{3,1,0,2:T(2,128)} %copy.12) | data formatting | bytes 3670016 | tf_op jit(solution)/shard_map/reshape
  80.4 2.4 %convolution_reduce_fusion.2 = f32[1792]{0:T(1024)S(1)} fusion(f32[256,1]{0,1:T(1,128)S(1)} %bitcast.28, f32[256,1792]{1,0:T(8,128)} %reshape.48), kind=kOutput, calls=%fused_computation.5 | convolution fusion | flops 5505024 | bytes 1843200 | tf_op jit(solution)/shard_map/c,crk->rk/dot_general | solution.py:22
  82.9 0.7 broadcast_divide_fusion.2
  83.5 0.3 bitcast_reduce_fusion.1
  83.8 0.1 copy.14
  83.9 0.1 reduce_sum.51
  84.1 6.1 %psum.56 = f32[256]{0:T(256)S(1)} all-reduce(f32[256]{0:T(256)S(1)} %reduce_sum.51), channel_id=1, replica_groups=mesh['client_0'=4,'client_1'=8,'client_2'=4,'param'=2] {'client_0'}, use_global_device_ids=true, to_apply=%region_2.0 | all-reduce | flops 256 | bytes 2048 | tf_op jit(solution)/shard_map/psum | solution.py:18
  90.1 11.7 %psum.57 = f32[256]{0:T(256)S(1)} all-reduce(f32[256]{0:T(256)S(1)} %psum.56), channel_id=1, replica_groups=mesh['client_0'=4,'client_1'=8,'client_2'=4,'param'=2] {'client_1'}, use_global_device_ids=true, to_apply=%region_3.0 | all-reduce | flops 256 | bytes 2048 | tf_op jit(solution)/shard_map/psum | solution.py:18
  101.8 8.8 %psum.58 = f32[256]{0:T(256)S(1)} all-reduce(f32[256]{0:T(256)S(1)} %psum.57), channel_id=1, replica_groups=mesh['client_0'=4,'client_1'=8,'client_2'=4,'param'=2] {'client_2'}, use_global_device_ids=true, to_apply=%region_4.0 | all-reduce | flops 256 | bytes 2048 | tf_op jit(solution)/shard_map/psum | solution.py:18
  110.7 13.8 %psum.59 = f32[256]{0:T(256)S(1)} all-reduce(f32[256]{0:T(256)S(1)} %psum.58), channel_id=1, replica_groups=mesh['client_0'=4,'client_1'=8,'client_2'=4,'param'=2] {'param'}, use_global_device_ids=true, to_apply=%region_5.0 | all-reduce | flops 256 | bytes 2048 | tf_op jit(solution)/shard_map/psum | solution.py:18
  124.5 0.6 fusion.1
  125.1 2.4 %convolution_reduce_fusion.1 = f32[1792]{0:T(1024)S(1)} fusion(f32[256,1]{0,1:T(1,128)S(1)} %bitcast.27, f32[256,1792]{1,0:T(8,128)} %reshape.48), kind=kOutput, calls=%fused_computation.4 | convolution fusion | flops 5505024 | bytes 1843200 | tf_op jit(solution)/shard_map/c,crk->rk/dot_general | solution.py:22
  127.5 0.7 broadcast_divide_fusion.1
  128.2 0.3 bitcast_reduce_fusion
  128.4 0.1 copy.16
  128.6 0.1 reduce_sum.54
  128.7 7.7 %psum.60 = f32[256]{0:T(256)S(1)} all-reduce(f32[256]{0:T(256)S(1)} %reduce_sum.54), channel_id=1, replica_groups=mesh['client_0'=4,'client_1'=8,'client_2'=4,'param'=2] {'client_0'}, use_global_device_ids=true, to_apply=%region_8.0 | all-reduce | flops 256 | bytes 2048 | tf_op jit(solution)/shard_map/psum | solution.py:18
  136.4 11.0 %psum.61 = f32[256]{0:T(256)S(1)} all-reduce(f32[256]{0:T(256)S(1)} %psum.60), channel_id=1, replica_groups=mesh['client_0'=4,'client_1'=8,'client_2'=4,'param'=2] {'client_1'}, use_global_device_ids=true, to_apply=%region_9.0 | all-reduce | flops 256 | bytes 2048 | tf_op jit(solution)/shard_map/psum | solution.py:18
  147.4 6.2 %psum.62 = f32[256]{0:T(256)S(1)} all-reduce(f32[256]{0:T(256)S(1)} %psum.61), channel_id=1, replica_groups=mesh['client_0'=4,'client_1'=8,'client_2'=4,'param'=2] {'client_2'}, use_global_device_ids=true, to_apply=%region_10.0 | all-reduce | flops 256 | bytes 2048 | tf_op jit(solution)/shard_map/psum | solution.py:18
  153.6 9.8 %psum.63 = f32[256]{0:T(256)S(1)} all-reduce(f32[256]{0:T(256)S(1)} %psum.62), channel_id=1, replica_groups=mesh['client_0'=4,'client_1'=8,'client_2'=4,'param'=2] {'param'}, use_global_device_ids=true, to_apply=%region_11.0 | all-reduce | flops 256 | bytes 2048 | tf_op jit(solution)/shard_map/psum | solution.py:18
  163.4 0.6 fusion
  164.0 0.6 multiply_divide_fusion
  164.6 2.5 %convolution_reduce_fusion = f32[1792]{0:T(1024)S(1)} fusion(f32[256,1]{0,1:T(1,128)S(1)} %bitcast.26, f32[256,1792]{1,0:T(8,128)} %reshape.48), kind=kOutput, calls=%fused_computation.3 | convolution fusion | flops 5505024 | bytes 1843200 | tf_op jit(solution)/shard_map/c,crk->rk/dot_general | solution.py:22
  167.1 0.7 broadcast_divide_fusion
  167.7 0.6 div.43
  168.3 0.6 dynamic_slice.3
  (2 shorter events, 0.0 us)
Async XLA Ops:
  4.8 16.5 %copy-start.1 = (u32[256]{0:T(256)S(1)}, u32[256]{0:T(256)}, u32[]{:S(2)}) copy-start(u32[256]{0:T(256)} %constant.34) | copy-start | bytes 3076
  4.8 17.7 %copy-start = (s32[2]{0:T(128)S(1)}, s32[2]{0:T(128)}, u32[]{:S(2)}) copy-start(s32[2]{0:T(128)} %param.3) | copy-start | bytes 28
  4.8 69.4 %all-to-all-start = ((f32[2,128,1792]{2,0,1:T(2,128)}), f32[2,128,1792]{2,0,1:T(2,128)S(1)}, u32[]{:S(2)}, u32[]{:S(2)}) async-start(f32[2,128,1792]{2,0,1:T(2,128)} %copy.10), calls=%async_computation | async-start | bytes 3670016 | tf_op jit(solution)/shard_map/all_to_all | solution.py:28
where the time goes:
time: 169 us
  blocking collectives  126 us (75%)
  starting transfers between devices  16.5 us (10%)
  local copies, waits for them, and re-layouts  12.9 us (8%)
  matrix products  7.35 us (4%)
  other arithmetic  4.95 us (3%)
    psum x8, blocking collectives, by_axis(): return functools.reduce(lax.psum, axes, shard)  75 us
    unnamed x1, blocking collectives  50.8 us
    all_to_all x1, starting transfers between devices, local(): lax.all_to_all(updates, CLIENT, split_axis=1, concat_axis=0, tiled=True)  16.5 us
    dot_general x3, matrix products, weighted_sum(): jnp.einsum('c,crk->rk', weights, updates, precision=lax.Precision.HIGHEST)  7.35 us
    unnamed x8, local copies, waits for them, and re-layouts  5.01 us
    reshape x1, local copies, waits for them, and re-layouts  3.41 us
  transfers between devices with their start and end apart: 1, of which 0 were waited for; matrix products, arithmetic and copies ran while one was open for 1% of the time, Pallas kernels for 0%

commit v1 on v0

v1 whole, which is shorter than its diff:
```python
import jax
import jax.numpy as jnp
from jax import lax
from jax.sharding import Mesh
from jax.sharding import PartitionSpec as P

ITERS = 2
SMOOTHING = 1e-06

CLIENT = ("y", "far", "pair", "x")
PLANE = ("y", "pair", "x")
PLANE_CORES = ("y", "pair", "x", "param")
LINE = ("far", "pair")

SUBLANES = 8
LANES = 128


def spread(value, axes):
    copies = jnp.broadcast_to(value[None], (lax.axis_size(axes), *value.shape))
    return lax.all_to_all(copies, axes, 0, 0, tiled=True)


def local(updates, sample_counts):
    clients, rows, columns = updates.shape
    ny, nfar, npair, nx = (lax.axis_size(a) for a in CLIENT)
    nz = nfar * npair
    plane = ny * npair * nx
    total_clients = clients * plane * nfar
    tiles = columns // npair // LANES

    blocks = updates.reshape(clients, ny, nz, nx, npair, tiles, LANES)
    blocks = blocks.transpose(1, 4, 3, 0, 5, 2, 6).reshape(plane, clients * tiles, nz, LANES)
    counts = sample_counts.astype(jnp.float32)
    counts = jnp.broadcast_to(jnp.repeat(counts, nz // clients)[None, None, :, None], (plane, 1, nz, LANES))
    held = lax.all_to_all(jnp.concatenate([blocks, counts], axis=1), PLANE, 0, 0, tiled=True)
    counts_f = held[:, clients * tiles, :: nz // clients, 0]
    held = held[:, : clients * tiles].reshape(plane, clients, tiles, nz, LANES)

    weights = counts_f
    for iteration in range(ITERS + 1):
        partial = jnp.sum(held * weights[:, :, None, None, None], axis=(0, 1))
        weight_sum = jnp.sum(weights)
        if iteration == ITERS:
            break
        sums = jnp.concatenate([partial, jnp.broadcast_to(weight_sum, (1, nz, LANES))])
        sums = jnp.sum(spread(sums, "far"), axis=0)
        median = sums[:tiles] / sums[tiles:]
        distance_sq = jnp.sum((held - median) ** 2, axis=(2, 3, 4)).reshape(-1)
        distance_sq = jnp.pad(distance_sq, (0, LANES - distance_sq.shape[0]))
        distance_sq = jnp.sum(spread(distance_sq, PLANE_CORES), axis=0)[: plane * clients]
        weights = counts_f / jnp.sqrt(distance_sq.reshape(plane, clients) + SMOOTHING)

    last = jnp.concatenate([partial.transpose(1, 0, 2), jnp.broadcast_to(weight_sum, (nz, 1, LANES))], axis=1)
    last = lax.all_to_all(last, LINE, 0, 0, tiled=True)
    last = jnp.sum(last.reshape(nfar, npair, tiles + 1, LANES), axis=0)
    weight_sum = last[0, tiles, 0]
    median = (last[:, :tiles] / weight_sum).reshape(1, columns)
    mine = lax.dynamic_slice_in_dim(weights, lax.axis_index(PLANE), 1, 0)[0]
    return median, total_clients * mine / weight_sum


def solution(mesh):
    finer = Mesh(
        mesh.devices.reshape(4, 4, 2, 4, mesh.shape["param"]),
        ("y", "far", "pair", "x", "param"),
    )
    return jax.shard_map(
        local,
        mesh=finer,
        in_specs=(P(CLIENT, None, "param"), P(CLIENT)),
        out_specs=(P(CLIENT, "param"), P(CLIENT)),
        check_vma=False,
    )
```

time: 169 us -> 120 us (0.71)
  blocking collectives: 126 us -> 89.3 us
  starting transfers between devices: 16.5 us -> 3.33 us
  matrix products: 7.35 us -> 0 us
  waiting for transfers between devices: 0.01 us -> 6.88 us
  other arithmetic: 4.95 us -> 9 us
  local copies, waits for them, and re-layouts: 12.9 us -> 10.1 us
    all_to_all x0 -> x5, blocking collectives: none -> 89.3 us  [the longest x4 54.9 us: spread(): return lax.all_to_all(copies, axes, 0, 0, tiled=True)]
    psum x8 -> x0, blocking collectives: 75 us -> none  [by_axis(): return functools.reduce(lax.psum, axes, shard)]
    unnamed x1 -> x0, blocking collectives: 50.8 us -> none
    all_to_all x1, starting transfers between devices: 16.5 us -> 3.33 us  [local(): last = lax.all_to_all(last, LINE, 0, 0, tiled=True)]
    dot_general x3 -> x0, matrix products: 7.35 us -> none  [weighted_sum(): jnp.einsum('c,crk->rk', weights, updates, precision=lax.Precision.HIGHEST)]
    all_to_all x1, waiting for transfers between devices: 0.01 us -> 6.88 us  [local(): last = lax.all_to_all(last, LINE, 0, 0, tiled=True)]
    unnamed x8 -> x3, local copies, waits for them, and re-layouts: 5.01 us -> 0.01 us
    reduce_sum x2 -> x15, other arithmetic: 0.53 us -> 3.48 us  [the longest x4 1.75 us: local(): distance_sq = jnp.sum((held - median) ** 2, axis=(2, 3, 4)).reshape(-1)]
  transfers between devices with their start and end apart: 1 -> 1, of which waited for: 0 -> 1; matrix products, arithmetic and copies ran while one was open for 1% -> 0% of each run, Pallas kernels for 0% -> 0%
where the time goes in v1:
time: 120 us
  blocking collectives  89.3 us (74%)
  local copies, waits for them, and re-layouts  10.1 us (8%)
  other arithmetic  9 us (8%)
  waiting for transfers between devices  6.88 us (6%)
  starting transfers between devices  3.33 us (3%)
    all_to_all x4, blocking collectives, spread(): return lax.all_to_all(copies, axes, 0, 0, tiled=True)  54.9 us
    all_to_all x1, blocking collectives, local(): lax.all_to_all(jnp.concatenate([blocks, counts], axis=1), PLANE, 0, 0, ti...  34.4 us
    all_to_all x1, waiting for transfers between devices, local(): last = lax.all_to_all(last, LINE, 0, 0, tiled=True)  6.88 us
    all_to_all x1, starting transfers between devices, local(): last = lax.all_to_all(last, LINE, 0, 0, tiled=True)  3.33 us
  transfers between devices with their start and end apart: 1, of which 1 were waited for; matrix products, arithmetic and copies ran while one was open for 0% of the time, Pallas kernels for 0%

profile of v1, /device:TPU:1, one launch (start us, length us, event | category | flops | bytes accessed | tf_op | source)
XLA Modules:
  0.0 119.5 jit_solution(17546660605080536790)
XLA Ops:
  0.6 1.8 %reshape.109 = f32[2,4,8,4,2,7,128]{6,5,4,3,2,1,0:T(8,128)S(1)} reshape(f32[2,128,1792]{2,1,0:T(8,128)} %param.2) | data formatting | bytes 3670016 | tf_op jit(solution)/shard_map/reshape | solution.py:32
  2.4 0.0 copy-start
  2.4 2.3 %copy.37 = f32[4,2,4,2,7,8,128]{6,5,4,3,2,1,0:T(8,128)} copy(f32[4,2,4,2,7,8,128]{6,4,1,2,5,0,3:T(8,128)S(1)} %bitcast.31) | data formatting | bytes 3670016 | tf_op jit(solution)/shard_map/transpose | solution.py:33
  4.8 0.0 copy-done
  4.8 0.1 broadcast_in_dim.14
  4.8 0.1 broadcast_in_dim.15
  4.9 0.1 broadcast_in_dim.16
  5.0 1.6 %pad_maximum_fusion = f32[32,15,8,128]{3,2,1,0:T(8,128)S(1)} fusion(f32[32,1,8,128]{3,2,1,0:T(8,128)S(1)} %broadcast_in_dim.16, f32[32,14,8,128]{3,2,1,0:T(8,128)} %bitcast.32), kind=kLoop, calls=%fused_computation | loop fusion | flops 491520 | bytes 3932160 | tf_op jit(solution)/shard_map/concatenate | solution.py:36
  6.6 34.4 %all_to_all.32 = f32[32,15,8,128]{3,2,1,0:T(8,128)S(1)} all-to-all(f32[32,15,8,128]{3,2,1,0:T(8,128)S(1)} %pad_maximum_fusion), channel_id=1, replica_groups=mesh['y'=4,'far'=4,'pair'=2,'x'=4,'param'=2] {'y','pair','x'}, dimensions={0} | all-to-all | bytes 3932160 | tf_op jit(solution)/shard_map/all_to_all | solution.py:36
  41.1 0.7 slice.53
  41.7 0.1 copy.38
  41.8 0.1 copy.39
  41.9 0.6 reduce_sum.155
  42.6 0.5 multiply_reduce_fusion.4
  43.1 0.7 concatenate.13
  43.8 14.3 %all_to_all.33 = f32[4,8,8,128]{3,2,1,0:T(8,128)S(1)} all-to-all(f32[4,8,8,128]{3,2,1,0:T(8,128)S(1)} %broadcast_in_dim.17), channel_id=1, replica_groups=mesh['y'=4,'far'=4,'pair'=2,'x'=4,'param'=2] {'far'}, dimensions={0} | all-to-all | bytes 262144 | tf_op jit(solution)/shard_map/all_to_all | solution.py:21
  58.2 0.9 multiply_reduce_fusion.3
  59.0 0.1 copy.40
  59.1 0.1 copy.41
  59.2 0.1 reshape.111
  59.4 16.7 %all_to_all.34 = f32[64,1,128]{2,1,0:T(1,128)S(1)} all-to-all(f32[64,1,128]{2,1,0:T(1,128)S(1)} %broadcast_in_dim.18), channel_id=1, replica_groups=mesh['y'=4,'far'=4,'pair'=2,'x'=4,'param'=2] {'y','pair','x','param'}, dimensions={0} | all-to-all | bytes 65536 | tf_op jit(solution)/shard_map/all_to_all | solution.py:21
  76.1 0.1 sqrt.11
  76.2 0.1 copy.43
  76.3 0.6 fusion.2
  76.9 0.1 copy.44
  77.0 0.5 multiply_reduce_fusion.2
  77.6 0.7 concatenate.14
  78.2 9.7 %all_to_all.35 = f32[4,8,8,128]{3,2,1,0:T(8,128)S(1)} all-to-all(f32[4,8,8,128]{3,2,1,0:T(8,128)S(1)} %broadcast_in_dim.19), channel_id=1, replica_groups=mesh['y'=4,'far'=4,'pair'=2,'x'=4,'param'=2] {'far'}, dimensions={0} | all-to-all | bytes 262144 | tf_op jit(solution)/shard_map/all_to_all | solution.py:21
  88.0 0.9 multiply_reduce_fusion.1
  88.9 0.1 copy.45
  89.0 0.1 copy.46
  89.1 0.1 reshape.112
  89.2 14.2 %all_to_all.36 = f32[64,1,128]{2,1,0:T(1,128)S(1)} all-to-all(f32[64,1,128]{2,1,0:T(1,128)S(1)} %broadcast_in_dim.20), channel_id=1, replica_groups=mesh['y'=4,'far'=4,'pair'=2,'x'=4,'param'=2] {'y','pair','x','param'}, dimensions={0} | all-to-all | bytes 65536 | tf_op jit(solution)/shard_map/all_to_all | solution.py:21
  103.4 0.1 sqrt.13
  103.6 0.1 copy.48
  103.6 0.6 fusion.1
  104.3 0.1 copy.49
  104.3 0.5 multiply_reduce_fusion
  104.9 1.3 %concatenate.15.clone = f32[8,8,128]{2,1,0:T(8,128)} pad(f32[8,7,128]{2,1,0:T(8,128)S(1)} %copy.51, f32[]{:T(128)} %get-tuple-element.2), padding=0_0x0_1x0_0 | pad | bytes 61444 | tf_op jit(solution)/shard_map/concatenate | solution.py:54
  106.2 3.3 %all-to-all-start.5 = ((f32[8,8,128]{2,1,0:T(8,128)}), f32[8,8,128]{2,1,0:T(8,128)S(1)}, u32[]{:S(2)}, u32[]{:S(2)}) async-start(f32[8,8,128]{2,1,0:T(8,128)} %concatenate.15.clone), calls=%async_computation.5 | async-start | bytes 65536 | tf_op jit(solution)/shard_map/all_to_all | solution.py:55
  109.5 6.9 %all-to-all-done.5 = f32[8,8,128]{2,1,0:T(8,128)S(1)} async-done(((f32[8,8,128]{2,1,0:T(8,128)}), f32[8,8,128]{2,1,0:T(8,128)S(1)}, u32[]{:S(2)}, u32[]{:S(2)}) %all-to-all-start.5) | async-done | bytes 32800 | tf_op jit(solution)/shard_map/all_to_all | solution.py:55
  116.4 0.5 slice.68
  116.9 0.6 slice_divide_fusion.2
  117.6 1.3 %fusion = f32[2]{0:T(128)} fusion(f32[32,2]{0,1:T(2,128)S(1)} %get-tuple-element.3, s32[]{:T(128)S(6)} %select_n.3, f32[]{:T(128)} %bitcast.14), kind=kLoop, calls=%fused_computation.12 | loop fusion | flops 4 | bytes 24 | tf_op jit(solution)/shard_map/div | solution.py:60
  118.9 0.6 reshape.114
  (34 shorter events, 0.3 us)
Async XLA Ops:
  2.4 2.3 %copy-start = (s32[2]{0:T(128)S(1)}, s32[2]{0:T(128)}, u32[]{:S(2)}) copy-start(s32[2]{0:T(128)} %param.3) | copy-start | bytes 28
  106.2 10.2 %all-to-all-start.5 = ((f32[8,8,128]{2,1,0:T(8,128)}), f32[8,8,128]{2,1,0:T(8,128)S(1)}, u32[]{:S(2)}, u32[]{:S(2)}) async-start(f32[8,8,128]{2,1,0:T(8,128)} %concatenate.15.clone), calls=%async_computation.5 | async-start | bytes 65536 | tf_op jit(solution)/shard_map/all_to_all | solution.py:55

commit v2 on v1

v2 whole, which is shorter than its diff:
```python
import functools

import jax
import jax.numpy as jnp
from jax import lax
from jax.experimental import pallas as pl
from jax.experimental.pallas import tpu as pltpu
from jax.sharding import Mesh
from jax.sharding import PartitionSpec as P

ITERS = 2
SMOOTHING = 1e-06

CLIENT = ("y", "far", "pair", "x")
PLANE = ("y", "pair", "x")
PLANE_CORES = ("y", "pair", "x", "param")
LINE = ("far", "pair")

SUB = 8
LANES = 128
VMEM = pl.BlockSpec(memory_space=pltpu.VMEM)
HBM = pl.BlockSpec(memory_space=pltpu.HBM)


def call(body, outs, in_specs, name, scratch=()):
    return pl.pallas_call(
        body,
        out_shape=outs,
        in_specs=in_specs,
        out_specs=jax.tree.map(lambda _: VMEM, outs),
        scratch_shapes=scratch,
        compiler_params=pltpu.CompilerParams(vmem_limit_bytes=8 << 20),
        name=name,
    )


def f32(*shape):
    return jax.ShapeDtypeStruct(shape, jnp.float32)


def wide(row, rows=SUB):
    return jnp.broadcast_to(row, (rows, LANES))


def pack_body(ny, nx, npair, tiles, u_hbm, counts_hbm, out, buf, counts, sems, counts_sem):
    clients, rows, _ = u_hbm.shape
    span = rows // ny

    def copy(k, j):
        n = k * npair * tiles + j
        return pltpu.make_async_copy(u_hbm.at[k, :, pl.ds(j * LANES, LANES)], buf.at[n], sems.at[n])

    fetch = pltpu.make_async_copy(counts_hbm, counts, counts_sem)
    fetch.start()
    for k in range(clients):
        for j in range(npair * tiles):
            copy(k, j).start()
    fetch.wait()
    upper = lax.broadcasted_iota(jnp.int32, (SUB, LANES), 0) >= SUB // 2
    tile = jnp.where(upper, counts[1], counts[0]).astype(jnp.float32)
    for p in range(ny * npair * nx):
        out[p, clients * tiles] = tile
    for k in range(clients):
        for j in range(npair * tiles):
            h, t = divmod(j, tiles)
            copy(k, j).wait()
            for y in range(ny):
                for x in range(nx):
                    part = buf[k * npair * tiles + j, pl.ds(y * span + x, SUB, stride=nx), :]
                    out[(y * npair + h) * nx + x, k * tiles + t] = part


def weighted(held, weights, tiles):
    plane = held.shape[0]

    def step(src, accs):
        accs = list(accs)
        for k in range(2):
            w = wide(weights[pl.ds(k * plane + src, 1), :])
            for t in range(tiles):
                accs[t] = accs[t] + w * held[src, k * tiles + t]
            accs[tiles] = accs[tiles] + w
        return tuple(accs)

    zero = jnp.zeros((SUB, LANES), jnp.float32)
    return lax.fori_loop(0, plane, step, (zero,) * (tiles + 1), unroll=8)


def take_counts(held, counts, tiles):
    plane = held.shape[0]
    for src in range(plane):
        for k in range(2):
            counts[pl.ds(k * plane + src, 1), :] = held[src, 2 * tiles, pl.ds(k * SUB // 2, 1), :]


def reweigh(held, dist, weights, tiles):
    plane = held.shape[0]
    take_counts(held, weights, tiles)
    total = jnp.sum(dist[:, 0, :], axis=0, keepdims=True)
    column = wide(total, LANES).T[: 2 * plane]
    weights[...] = weights[...] / jnp.sqrt(column + SMOOTHING)


def start_body(tiles, held, out, weights):
    take_counts(held, weights, tiles)
    sums = weighted(held, weights, tiles)
    for f in range(out.shape[0]):
        for t in range(tiles + 1):
            out[f, t] = sums[t]


def again_body(tiles, held, dist, out, weights):
    reweigh(held, dist, weights, tiles)
    sums = weighted(held, weights, tiles)
    for f in range(out.shape[0]):
        for t in range(tiles + 1):
            out[f, t] = sums[t]


def last_body(tiles, held, dist, out, mine, weights):
    plane = held.shape[0]
    reweigh(held, dist, weights, tiles)
    sums = weighted(held, weights, tiles)
    nz = out.shape[0] // SUB
    for t in range(tiles + 1):
        out[pl.ds(t, nz, stride=SUB), :] = sums[t]
    me = lax.axis_index(PLANE)
    for k in range(2):
        mine[pl.ds(k * SUB // 2, SUB // 2), :] = wide(weights[pl.ds(k * plane + me, 1), :], SUB // 2)


def distance_body(tiles, held, sums, out, rows):
    plane = held.shape[0]
    whole = [functools.reduce(jnp.add, [sums[f, t] for f in range(sums.shape[0])]) for t in range(tiles + 1)]
    median = [whole[t] / whole[tiles] for t in range(tiles)]

    def step(src, carry):
        for k in range(2):
            acc = None
            for t in range(tiles):
                diff = held[src, k * tiles + t] - median[t]
                acc = diff * diff if acc is None else acc + diff * diff
            rows[pl.ds(pl.multiple_of((k * plane + src) * SUB, SUB), SUB), :] = acc
        return carry

    lax.fori_loop(0, plane, step, 0, unroll=8)
    clients = 2 * plane
    lanes = []
    for g in range(clients // SUB):
        parts = [rows[pl.ds(g * SUB * SUB + s, SUB, stride=SUB), :] for s in range(SUB)]
        lanes.append(functools.reduce(jnp.add, parts))
    lanes = jnp.concatenate(lanes + [jnp.zeros((LANES - clients, LANES), jnp.float32)], axis=0)
    out[...] = jnp.sum(lanes.T, axis=0, keepdims=True)


def finish_body(total_clients, tiles, got, mine, median, shares):
    nfar = got.shape[0] // 2
    halves = []
    for h in range(2):
        halves.append(functools.reduce(jnp.add, [got[f * 2 + h] for f in range(nfar)]))
    total = halves[0][tiles : tiles + 1]
    for h in range(2):
        part = halves[h] / total
        for t in range(tiles):
            median[:, pl.ds((h * tiles + t) * LANES, LANES)] = part[t : t + 1]
    share = total_clients * mine[...] / total
    lane = lax.broadcasted_iota(jnp.int32, (1, LANES), 1)
    share = jnp.where(lane == 0, share[:1], share[SUB // 2 : SUB // 2 + 1])
    shares[...] = share[0, : shares.shape[0]]


def local(updates, sample_counts):
    clients, rows, columns = updates.shape
    ny, nfar, npair, nx = (lax.axis_size(a) for a in CLIENT)
    nz = nfar * npair
    plane = ny * npair * nx
    tiles = columns // npair // LANES
    bind = functools.partial

    held = call(
        bind(pack_body, ny, nx, npair, tiles),
        f32(plane, clients * tiles + 1, nz, LANES),
        [HBM, HBM],
        "pack",
        scratch=[
            pltpu.VMEM((clients * npair * tiles, rows, LANES), jnp.float32),
            pltpu.SMEM((clients,), jnp.int32),
            pltpu.SemaphoreType.DMA((clients * npair * tiles,)),
            pltpu.SemaphoreType.DMA,
        ],
    )(*(pltpu.with_memory_space_constraint(a, pltpu.HBM) for a in (updates, sample_counts)))
    held = lax.all_to_all(held, PLANE, 0, 0, tiled=True)

    rows_of_weights = [pltpu.VMEM((clients * plane, LANES), jnp.float32)]
    payload = f32(nfar, tiles + 1, nz, LANES)
    sums = call(bind(start_body, tiles), payload, [VMEM], "start", scratch=rows_of_weights)(held)
    for iteration in range(ITERS):
        sums = lax.all_to_all(sums, "far", 0, 0, tiled=True)
        dist = call(
            bind(distance_body, tiles),
            f32(1, LANES),
            [VMEM, VMEM],
            "distance",
            scratch=[pltpu.VMEM((clients * plane * SUB, LANES), jnp.float32)],
        )(held, sums)
        dist = jnp.broadcast_to(dist[None], (plane * lax.axis_size("param"), 1, LANES))
        dist = lax.all_to_all(dist, PLANE_CORES, 0, 0, tiled=True)
        if iteration < ITERS - 1:
            sums = call(bind(again_body, tiles), payload, [VMEM, VMEM], "again", scratch=rows_of_weights)(held, dist)
    last, mine = call(
        bind(last_body, tiles),
        (f32(nz * SUB, LANES), f32(SUB, LANES)),
        [VMEM, VMEM],
        "last",
        scratch=rows_of_weights,
    )(held, dist)
    last = lax.all_to_all(last.reshape(nz, SUB, LANES), LINE, 0, 0, tiled=True)
    median, shares = call(
        bind(finish_body, clients * plane * nfar, tiles),
        (f32(1, columns), f32(clients)),
        [VMEM, VMEM],
        "finish",
    )(last, mine)
    return median, shares


def solution(mesh):
    finer = Mesh(
        mesh.devices.reshape(4, 4, 2, 4, mesh.shape["param"]),
        ("y", "far", "pair", "x", "param"),
    )
    return jax.shard_map(
        local,
        mesh=finer,
        in_specs=(P(CLIENT, None, "param"), P(CLIENT)),
        out_specs=(P(CLIENT, "param"), P(CLIENT)),
        check_vma=False,
    )
```

time: 120 us -> 104 us (0.87)
  local copies, waits for them, and re-layouts: 10.1 us -> 0.04 us
  blocking collectives: 89.3 us -> 98.7 us
  other arithmetic: 9 us -> 0 us
  waiting for transfers between devices: 6.88 us -> 0 us
  Pallas kernels: 0 us -> 3.8 us
  starting transfers between devices: 3.33 us -> 0 us
    all_to_all x5 -> x6, blocking collectives: 89.3 us -> 98.7 us  [the longest x1 34.4 us: local(): held = lax.all_to_all(held, PLANE, 0, 0, tiled=True)]
    all_to_all x1 -> x0, waiting for transfers between devices: 6.88 us -> none  [local(): last = lax.all_to_all(last, LINE, 0, 0, tiled=True)]
    reduce_sum x18 -> x0, other arithmetic: 5.35 us -> none  [the longest x3 1.87 us: local(): weight_sum = jnp.sum(weights)]
    pallas_call x0 -> x7, Pallas kernels: none -> 3.8 us  [the longest x1 1.76 us: local(): call(bind(pack_body, ny, nx, npair, tiles), f32(plane, clients * tiles +...]
    all_to_all x1 -> x0, starting transfers between devices: 3.33 us -> none  [local(): last = lax.all_to_all(last, LINE, 0, 0, tiled=True)]
    reshape x4 -> x0, local copies, waits for them, and re-layouts: 2.62 us -> none  [the longest x1 1.8 us: local(): blocks = updates.reshape(clients, ny, nz, nx, npair, tiles, LANES)]
    concatenate x3 -> x0, local copies, waits for them, and re-layouts: 2.55 us -> none  [the longest x2 1.3 us: local(): jnp.concatenate([partial, jnp.broadcast_to(weight_sum, (1, nz, LANES))])]
    transpose x1 -> x0, local copies, waits for them, and re-layouts: 2.32 us -> none  [local(): blocks.transpose(1, 4, 3, 0, 5, 2, 6)]
  transfers between devices with their start and end apart: 1 -> 0, of which waited for: 1 -> 0; matrix products, arithmetic and copies ran while one was open for 0% -> 0% of each run, Pallas kernels for 0% -> 0%
where the time goes in v2:
time: 104 us; the launch traced here: 103 us
  blocking collectives  98.7 us (95%)
  Pallas kernels  3.8 us (4%)
    all_to_all x1, blocking collectives, local(): held = lax.all_to_all(held, PLANE, 0, 0, tiled=True)  34.4 us
    all_to_all x2, blocking collectives, local(): dist = lax.all_to_all(dist, PLANE_CORES, 0, 0, tiled=True)  30.9 us
    all_to_all x2, blocking collectives, local(): sums = lax.all_to_all(sums, 'far', 0, 0, tiled=True)  24 us
    all_to_all x1, blocking collectives, local(): last = lax.all_to_all(last.reshape(nz, SUB, LANES), LINE, 0, 0, tiled=True)  9.33 us

profile of v2, /device:TPU:1, one launch (start us, length us, event | category | flops | bytes accessed | tf_op | source)
XLA Modules:
  0.0 103.2 jit_solution(2237685562437856555)
XLA Ops:
  0.6 1.8 %pack.1 = f32[32,15,8,128]{3,2,1,0:T(8,128)S(1)} custom-call(f32[2,128,1792]{2,1,0:T(8,128)} %u_hbm.1, s32[2]{0:T(128)} %counts_hbm.1), custom_call_target="tpu_custom_call" | custom-call | tf_op jit(solution)/shard_map/pack/pallas_call | solution.py:180
  2.4 34.4 %all_to_all.30.held = f32[32,15,8,128]{3,2,1,0:T(8,128)S(1)} all-to-all(f32[32,15,8,128]{3,2,1,0:T(8,128)S(1)} %pack.1), channel_id=1, replica_groups=mesh['y'=4,'far'=4,'pair'=2,'x'=4,'param'=2] {'y','pair','x'}, dimensions={0} | all-to-all | bytes 3932160 | tf_op jit(solution)/shard_map/all_to_all | solution.py:192
  36.8 0.2 start.1
  37.0 14.3 %all_to_all.31.sums = f32[4,8,8,128]{3,2,1,0:T(8,128)S(1)} all-to-all(f32[4,8,8,128]{3,2,1,0:T(8,128)S(1)} %start.1), channel_id=1, replica_groups=mesh['y'=4,'far'=4,'pair'=2,'x'=4,'param'=2] {'far'}, dimensions={0} | all-to-all | bytes 262144 | tf_op jit(solution)/shard_map/all_to_all | solution.py:198
  51.3 0.3 distance.2
  51.7 16.7 %all_to_all.32.dist = f32[64,1,128]{2,1,0:T(1,128)S(1)} all-to-all(f32[64,1,128]{2,1,0:T(1,128)S(1)} %broadcast_in_dim.17), channel_id=1, replica_groups=mesh['y'=4,'far'=4,'pair'=2,'x'=4,'param'=2] {'y','pair','x','param'}, dimensions={0} | all-to-all | bytes 65536 | tf_op jit(solution)/shard_map/all_to_all | solution.py:207
  68.4 0.3 again.1
  68.7 9.7 %all_to_all.33.sums = f32[4,8,8,128]{3,2,1,0:T(8,128)S(1)} all-to-all(f32[4,8,8,128]{3,2,1,0:T(8,128)S(1)} %again.1), channel_id=1, replica_groups=mesh['y'=4,'far'=4,'pair'=2,'x'=4,'param'=2] {'far'}, dimensions={0} | all-to-all | bytes 262144 | tf_op jit(solution)/shard_map/all_to_all | solution.py:198
  78.4 0.3 distance.3
  78.8 14.2 %all_to_all.34.dist = f32[64,1,128]{2,1,0:T(1,128)S(1)} all-to-all(f32[64,1,128]{2,1,0:T(1,128)S(1)} %broadcast_in_dim.19), channel_id=1, replica_groups=mesh['y'=4,'far'=4,'pair'=2,'x'=4,'param'=2] {'y','pair','x','param'}, dimensions={0} | all-to-all | bytes 65536 | tf_op jit(solution)/shard_map/all_to_all | solution.py:207
  92.9 0.3 last.1
  93.2 9.3 %all_to_all.35.got = f32[8,8,128]{2,1,0:T(8,128)S(1)} all-to-all(f32[8,8,128]{2,1,0:T(8,128)S(1)} %bitcast.3), channel_id=1, replica_groups=mesh['y'=4,'far'=4,'pair'=2,'x'=4,'param'=2] {'far','pair'}, dimensions={0} | all-to-all | bytes 65536 | tf_op jit(solution)/shard_map/all_to_all | solution.py:217
  102.6 0.6 finish.1
  (2 shorter events, 0.0 us)

commit v3 on v1

v3 whole, which is shorter than its diff:
```python
import functools

import jax
import jax.numpy as jnp
from jax import lax
from jax.experimental import pallas as pl
from jax.experimental.pallas import tpu as pltpu
from jax.sharding import Mesh
from jax.sharding import PartitionSpec as P

ITERS = 2
SMOOTHING = 1e-06

CLIENT = ("y", "far", "pair", "x")
PLANE = ("y", "pair", "x")
PLANE_CORES = ("y", "pair", "x", "param")
LINE = ("far", "pair")
GROUPS = ((0, 2, 5, 7), (1, 3, 4, 6))

SUB = 8
HALF = SUB // 2
LANES = 128
VMEM = pl.BlockSpec(memory_space=pltpu.VMEM)
HBM = pl.BlockSpec(memory_space=pltpu.HBM)


def call(body, outs, in_specs, name, scratch=()):
    return pl.pallas_call(
        body,
        out_shape=outs,
        in_specs=in_specs,
        out_specs=jax.tree.map(lambda _: VMEM, outs),
        scratch_shapes=scratch,
        compiler_params=pltpu.CompilerParams(vmem_limit_bytes=8 << 20),
        name=name,
    )


def f32(*shape):
    return jax.ShapeDtypeStruct(shape, jnp.float32)


def sublane():
    return lax.broadcasted_iota(jnp.int32, (SUB, LANES), 0)


def pack_body(tiles, u_hbm, counts_hbm, out, buf, counts, sems, counts_sem):
    clients, ny, span, _ = u_hbm.shape
    nx = span // SUB

    def copy(k, j):
        src = u_hbm.at[k, :, :, pl.ds(j * LANES, LANES)]
        return pltpu.make_async_copy(src, buf.at[j, :, pl.ds(k * span, span), :], sems.at[k, j])

    fetch = pltpu.make_async_copy(counts_hbm, counts, counts_sem)
    fetch.start()
    for j in range(tiles):
        for k in range(clients):
            copy(k, j).start()
    row = sublane()
    flip = (lax.axis_index("far") >= 2).astype(jnp.int32)
    mask = ((row >> 1) & 1) == flip
    fetch.wait()
    tile = jnp.where(row < HALF, counts[0], counts[1]).astype(jnp.float32)
    for p in range(ny * 2 * nx):
        out[p, tiles] = tile
    for j in range(tiles):
        for k in range(clients):
            copy(k, j).wait()
        for y in range(ny):
            for x in range(nx):
                even = buf[j, y, pl.ds(x, SUB, stride=2 * nx), :]
                odd = buf[j, y, pl.ds(nx + x, SUB, stride=2 * nx), :]
                out[(y * 2) * nx + x, j] = jnp.where(mask, even, odd)
                out[(y * 2 + 1) * nx + x, j] = jnp.where(mask, odd, even)


def weighted(held, weigh):
    plane, tiles = held.shape[0], held.shape[1] - 1

    def step(src, accs):
        w = weigh(src)
        sums = [accs[t] + w * held[src, t] for t in range(tiles)]
        return (*sums, accs[tiles] + w)

    zero = jnp.zeros((SUB, LANES), jnp.float32)
    accs = lax.fori_loop(0, plane, step, (zero,) * (tiles + 1), unroll=8)
    return [a + pltpu.roll(a, HALF, 0) for a in accs]


def weigh_by_count(held):
    return lambda src: held[src, held.shape[1] - 1]


def weigh_by_distance(held, dist, spread):
    clients = 2 * held.shape[0]
    total = jnp.sum(dist[:, 0, :], axis=0, keepdims=True)
    column = jnp.broadcast_to(total, (LANES, LANES)).T[:clients]
    for i in range(HALF):
        spread[pl.ds(i, clients, stride=HALF), :] = column
    counts = weigh_by_count(held)

    def weigh(src):
        at = pl.ds(pl.multiple_of(src * SUB, SUB), SUB)
        return counts(src) / jnp.sqrt(spread[at, :] + SMOOTHING)

    return weigh


def give_sums(sums, out):
    top = sublane() < HALF
    tiles = len(sums) - 1
    for g in range(out.shape[0]):
        for t in range(tiles // 2):
            out[g, t] = jnp.where(top, sums[2 * t], sums[2 * t + 1])
        out[g, tiles // 2] = sums[tiles]


def start_body(held, out):
    give_sums(weighted(held, weigh_by_count(held)), out)


def again_body(held, dist, out, spread):
    give_sums(weighted(held, weigh_by_distance(held, dist, spread)), out)


def last_body(held, dist, out, mine, spread):
    weigh = weigh_by_distance(held, dist, spread)
    sums = weighted(held, weigh)
    deep = out.shape[0] // HALF
    for t in range(deep):
        out[pl.ds(t, HALF, stride=deep), :] = sums[min(t, len(sums) - 1)][:HALF]
    mine[...] = weigh(lax.axis_index(PLANE))


def distance_body(held, sums, out, rows):
    plane, tiles = held.shape[0], held.shape[1] - 1
    whole = [functools.reduce(jnp.add, [sums[g, t] for g in range(sums.shape[0])]) for t in range(tiles // 2 + 1)]
    top = sublane() < HALF
    median = []
    for t in range(tiles // 2):
        m = whole[t] / whole[tiles // 2]
        r = pltpu.roll(m, HALF, 0)
        median += [jnp.where(top, m, r), jnp.where(top, r, m)]

    def step(src, carry):
        acc = None
        for t in range(tiles):
            diff = held[src, t] - median[t]
            acc = diff * diff if acc is None else acc + diff * diff
        rows[pl.ds(pl.multiple_of(src * SUB, SUB), SUB), :] = acc
        return carry

    lax.fori_loop(0, plane, step, 0, unroll=8)
    clients = 2 * plane
    lanes = []
    for g in range(clients // SUB):
        parts = [rows[pl.ds(g * SUB * HALF + i, SUB, stride=HALF), :] for i in range(HALF)]
        lanes.append(functools.reduce(jnp.add, parts))
    lanes = jnp.concatenate(lanes + [jnp.zeros((LANES - clients, LANES), jnp.float32)], axis=0)
    out[...] = jnp.sum(lanes.T, axis=0, keepdims=True)


def finish_body(total_clients, got, mine, median, shares):
    tiles = median.shape[1] // LANES
    whole = functools.reduce(jnp.add, [got[g] for g in range(got.shape[0])])
    total = whole[tiles : tiles + 1]
    part = whole / total
    for t in range(tiles):
        median[:, pl.ds(t * LANES, LANES)] = part[t : t + 1]
    share = total_clients * mine[...] / total
    lane = lax.broadcasted_iota(jnp.int32, (1, LANES), 1)
    share = jnp.where(lane == 0, share[:1], share[HALF : HALF + 1])
    shares[...] = share[0, : shares.shape[0]]


def local(updates, sample_counts):
    clients, rows, columns = updates.shape
    ny, nfar, npair, nx = (lax.axis_size(a) for a in CLIENT)
    plane = ny * npair * nx
    tiles = columns // LANES
    deep = 2 * SUB

    updates = updates.reshape(clients, ny, rows // ny, columns)
    held = call(
        functools.partial(pack_body, tiles),
        f32(plane, tiles + 1, SUB, LANES),
        [HBM, HBM],
        "pack",
        scratch=[
            pltpu.VMEM((tiles, ny, clients * (rows // ny), LANES), jnp.float32),
            pltpu.SMEM((clients,), jnp.int32),
            pltpu.SemaphoreType.DMA((clients, tiles)),
            pltpu.SemaphoreType.DMA,
        ],
    )(*(pltpu.with_memory_space_constraint(a, pltpu.HBM) for a in (updates, sample_counts)))
    held = lax.all_to_all(held, PLANE, 0, 0, tiled=True)

    per_row = [pltpu.VMEM((plane * SUB, LANES), jnp.float32)]
    payload = f32(nfar, tiles // 2 + 1, SUB, LANES)
    along_z = functools.partial(
        lax.all_to_all, axis_name=LINE, split_axis=0, concat_axis=0, tiled=True, axis_index_groups=GROUPS
    )
    sums = call(start_body, payload, [VMEM], "start")(held)
    for iteration in range(ITERS):
        dist = call(distance_body, f32(1, LANES), [VMEM, VMEM], "distance", scratch=per_row)(held, along_z(sums))
        dist = jnp.broadcast_to(dist[None], (plane * lax.axis_size("param"), 1, LANES))
        dist = lax.all_to_all(dist, PLANE_CORES, 0, 0, tiled=True)
        if iteration < ITERS - 1:
            sums = call(again_body, payload, [VMEM, VMEM], "again", scratch=per_row)(held, dist)
    last, mine = call(
        last_body, (f32(nfar * deep, LANES), f32(SUB, LANES)), [VMEM, VMEM], "last", scratch=per_row
    )(held, dist)
    median, shares = call(
        functools.partial(finish_body, clients * plane * nfar), (f32(1, columns), f32(clients)), [VMEM, VMEM], "finish"
    )(along_z(last.reshape(nfar, deep, LANES)), mine)
    return median, shares


def solution(mesh):
    finer = Mesh(
        mesh.devices.reshape(4, 4, 2, 4, mesh.shape["param"]),
        ("y", "far", "pair", "x", "param"),
    )
    return jax.shard_map(
        local,
        mesh=finer,
        in_specs=(P(CLIENT, None, "param"), P(CLIENT)),
        out_specs=(P(CLIENT, "param"), P(CLIENT)),
        check_vma=False,
    )
```

time: 120 us -> 101 us (0.84)
  local copies, waits for them, and re-layouts: 10.1 us -> 0.05 us
  other arithmetic: 9 us -> 0 us
  waiting for transfers between devices: 6.88 us -> 0 us
  blocking collectives: 89.3 us -> 95.5 us
  Pallas kernels: 0 us -> 3.93 us
  starting transfers between devices: 3.33 us -> 0 us
    all_to_all x1 -> x0, waiting for transfers between devices: 6.88 us -> none  [local(): last = lax.all_to_all(last, LINE, 0, 0, tiled=True)]
    all_to_all x5 -> x6, blocking collectives: 89.3 us -> 95.5 us  [the longest x1 34.4 us: local(): held = lax.all_to_all(held, PLANE, 0, 0, tiled=True)]
    reduce_sum x18 -> x0, other arithmetic: 5.35 us -> none  [the longest x3 1.87 us: local(): weight_sum = jnp.sum(weights)]
    pallas_call x0 -> x7, Pallas kernels: none -> 3.93 us  [the longest x1 1.81 us: local(): call(functools.partial(pack_body, tiles), f32(plane, tiles + 1, SUB, LANE...]
    all_to_all x1 -> x0, starting transfers between devices: 3.33 us -> none  [local(): last = lax.all_to_all(last, LINE, 0, 0, tiled=True)]
    reshape x4 -> x0, local copies, waits for them, and re-layouts: 2.62 us -> none  [the longest x1 1.8 us: local(): blocks = updates.reshape(clients, ny, nz, nx, npair, tiles, LANES)]
    concatenate x3 -> x0, local copies, waits for them, and re-layouts: 2.55 us -> none  [the longest x2 1.3 us: local(): jnp.concatenate([partial, jnp.broadcast_to(weight_sum, (1, nz, LANES))])]
    transpose x1 -> x0, local copies, waits for them, and re-layouts: 2.32 us -> none  [local(): blocks.transpose(1, 4, 3, 0, 5, 2, 6)]
  transfers between devices with their start and end apart: 1 -> 0, of which waited for: 1 -> 0; matrix products, arithmetic and copies ran while one was open for 0% -> 0% of each run, Pallas kernels for 0% -> 0%
where the time goes in v3:
time: 101 us; the launch traced here: 100 us
  blocking collectives  95.5 us (95%)
  Pallas kernels  3.93 us (4%)
    all_to_all x1, blocking collectives, local(): held = lax.all_to_all(held, PLANE, 0, 0, tiled=True)  34.4 us
    all_to_all x2, blocking collectives, local(): dist = lax.all_to_all(dist, PLANE_CORES, 0, 0, tiled=True)  31.3 us
    all_to_all x2, blocking collectives, local(): along_z(sums)  21.6 us
    all_to_all x1, blocking collectives, local(): along_z(last.reshape(nfar, deep, LANES))  8.17 us

profile of v3, /device:TPU:1, one launch (start us, length us, event | category | flops | bytes accessed | tf_op | source)
XLA Modules:
  0.0 100.2 jit_solution(2214870838645025430)
XLA Ops:
  0.6 1.8 %pack.1 = f32[32,15,8,128]{3,2,1,0:T(8,128)S(1)} custom-call(f32[2,4,32,1792]{3,2,1,0:T(8,128)} %bitcast.7, s32[2]{0:T(128)} %counts_hbm.1), custom_call_target="tpu_custom_call" | custom-call | tf_op jit(solution)/shard_map/pack/pallas_call | solution.py:185
  2.4 34.4 %all_to_all.30.held = f32[32,15,8,128]{3,2,1,0:T(8,128)S(1)} all-to-all(f32[32,15,8,128]{3,2,1,0:T(8,128)S(1)} %pack.1), channel_id=1, replica_groups=mesh['y'=4,'far'=4,'pair'=2,'x'=4,'param'=2] {'y','pair','x'}, dimensions={0} | all-to-all | bytes 3932160 | tf_op jit(solution)/shard_map/all_to_all | solution.py:197
  36.9 0.2 start.1
  37.0 12.5 %all_to_all.31.sums = f32[4,8,8,128]{3,2,1,0:T(8,128)S(1)} all-to-all(f32[4,8,8,128]{3,2,1,0:T(8,128)S(1)} %start.1), channel_id=1, replica_groups={{0,16,40,56},{8,24,32,48},{1,17,41,57},{9,25,33,49},{2,18,42,58},{10,26..., dimensions={0} | all-to-all | bytes 262144 | tf_op jit(solution)/shard_map/all_to_all | solution.py:206
  49.5 0.3 distance.2
  49.9 17.0 %all_to_all.32.dist = f32[64,1,128]{2,1,0:T(1,128)S(1)} all-to-all(f32[64,1,128]{2,1,0:T(1,128)S(1)} %broadcast_in_dim.17), channel_id=1, replica_groups=mesh['y'=4,'far'=4,'pair'=2,'x'=4,'param'=2] {'y','pair','x','param'}, dimensions={0} | all-to-all | bytes 65536 | tf_op jit(solution)/shard_map/all_to_all | solution.py:208
  66.9 0.4 again.1
  67.3 9.1 %all_to_all.33.sums = f32[4,8,8,128]{3,2,1,0:T(8,128)S(1)} all-to-all(f32[4,8,8,128]{3,2,1,0:T(8,128)S(1)} %again.1), channel_id=1, replica_groups={{0,16,40,56},{8,24,32,48},{1,17,41,57},{9,25,33,49},{2,18,42,58},{10,26..., dimensions={0} | all-to-all | bytes 262144 | tf_op jit(solution)/shard_map/all_to_all | solution.py:206
  76.4 0.3 distance.3
  76.7 14.3 %all_to_all.34.dist = f32[64,1,128]{2,1,0:T(1,128)S(1)} all-to-all(f32[64,1,128]{2,1,0:T(1,128)S(1)} %broadcast_in_dim.19), channel_id=1, replica_groups=mesh['y'=4,'far'=4,'pair'=2,'x'=4,'param'=2] {'y','pair','x','param'}, dimensions={0} | all-to-all | bytes 65536 | tf_op jit(solution)/shard_map/all_to_all | solution.py:208
  91.0 0.4 last.1
  91.4 8.2 %all_to_all.35.got = f32[4,16,128]{2,1,0:T(8,128)S(1)} all-to-all(f32[4,16,128]{2,1,0:T(8,128)S(1)} %bitcast.4), channel_id=1, replica_groups={{0,16,40,56},{8,24,32,48},{1,17,41,57},{9,25,33,49},{2,18,42,58},{10,26..., dimensions={0} | all-to-all | bytes 65536 | tf_op jit(solution)/shard_map/all_to_all | solution.py:216
  99.6 0.6 finish.1
  (2 shorter events, 0.0 us)

commit v4 on v3

--- a/solution.py
+++ b/solution.py
@@ -24,12 +24,12 @@
 HBM = pl.BlockSpec(memory_space=pltpu.HBM)
 
 
-def call(body, outs, in_specs, name, scratch=()):
+def call(body, outs, in_specs, name, scratch=(), out_specs=None):
     return pl.pallas_call(
         body,
         out_shape=outs,
         in_specs=in_specs,
-        out_specs=jax.tree.map(lambda _: VMEM, outs),
+        out_specs=jax.tree.map(lambda _: VMEM, outs) if out_specs is None else out_specs,
         scratch_shapes=scratch,
         compiler_params=pltpu.CompilerParams(vmem_limit_bytes=8 << 20),
         name=name,
@@ -44,7 +44,7 @@
     return lax.broadcasted_iota(jnp.int32, (SUB, LANES), 0)
 
 
-def pack_body(tiles, u_hbm, counts_hbm, out, buf, counts, sems, counts_sem):
+def pack_body(tiles, u_hbm, out_hbm, buf, out, sems, out_sems):
     clients, ny, span, _ = u_hbm.shape
     nx = span // SUB
 
@@ -52,18 +52,14 @@
         src = u_hbm.at[k, :, :, pl.ds(j * LANES, LANES)]
         return pltpu.make_async_copy(src, buf.at[j, :, pl.ds(k * span, span), :], sems.at[k, j])
 
-    fetch = pltpu.make_async_copy(counts_hbm, counts, counts_sem)
-    fetch.start()
+    def send(j):
+        return pltpu.make_async_copy(out.at[j], out_hbm.at[:, j], out_sems.at[j])
+
     for j in range(tiles):
         for k in range(clients):
             copy(k, j).start()
-    row = sublane()
     flip = (lax.axis_index("far") >= 2).astype(jnp.int32)
-    mask = ((row >> 1) & 1) == flip
-    fetch.wait()
-    tile = jnp.where(row < HALF, counts[0], counts[1]).astype(jnp.float32)
-    for p in range(ny * 2 * nx):
-        out[p, tiles] = tile
+    mask = ((sublane() >> 1) & 1) == flip
     for j in range(tiles):
         for k in range(clients):
             copy(k, j).wait()
@@ -71,12 +67,17 @@
             for x in range(nx):
                 even = buf[j, y, pl.ds(x, SUB, stride=2 * nx), :]
                 odd = buf[j, y, pl.ds(nx + x, SUB, stride=2 * nx), :]
-                out[(y * 2) * nx + x, j] = jnp.where(mask, even, odd)
-                out[(y * 2 + 1) * nx + x, j] = jnp.where(mask, odd, even)
+                out[j, (y * 2) * nx + x] = jnp.where(mask, even, odd)
+                out[j, (y * 2 + 1) * nx + x] = jnp.where(mask, odd, even)
+        if j:
+            send(j - 1).start()
+    send(tiles - 1).start()
+    for j in range(tiles):
+        send(j).wait()
 
 
 def weighted(held, weigh):
-    plane, tiles = held.shape[0], held.shape[1] - 1
+    plane, tiles = held.shape[0], held.shape[1]
 
     def step(src, accs):
         w = weigh(src)
@@ -88,23 +89,19 @@
     return [a + pltpu.roll(a, HALF, 0) for a in accs]
 
 
-def weigh_by_count(held):
-    return lambda src: held[src, held.shape[1] - 1]
-
-
-def weigh_by_distance(held, dist, spread):
-    clients = 2 * held.shape[0]
-    total = jnp.sum(dist[:, 0, :], axis=0, keepdims=True)
-    column = jnp.broadcast_to(total, (LANES, LANES)).T[:clients]
+def per_client(row, spread):
+    clients = spread.shape[0] // HALF
+    column = jnp.broadcast_to(row, (LANES, LANES)).T[:clients]
     for i in range(HALF):
         spread[pl.ds(i, clients, stride=HALF), :] = column
-    counts = weigh_by_count(held)
-
-    def weigh(src):
-        at = pl.ds(pl.multiple_of(src * SUB, SUB), SUB)
-        return counts(src) / jnp.sqrt(spread[at, :] + SMOOTHING)
-
-    return weigh
+    return lambda src: spread[pl.ds(pl.multiple_of(src * SUB, SUB), SUB), :]
+
+
+def weigh_by_distance(counts, dist, spread):
+    lane = lax.broadcasted_iota(jnp.int32, (1, LANES), 1)
+    total = jnp.sum(dist[:, 0, :], axis=0, keepdims=True)
+    weight = counts[...] / jnp.sqrt(jnp.where(lane < spread.shape[0] // HALF, total, 1.0) + SMOOTHING)
+    return per_client(weight, spread)
 
 
 def give_sums(sums, out):
@@ -116,16 +113,16 @@
         out[g, tiles // 2] = sums[tiles]
 
 
-def start_body(held, out):
-    give_sums(weighted(held, weigh_by_count(held)), out)
-
-
-def again_body(held, dist, out, spread):
-    give_sums(weighted(held, weigh_by_distance(held, dist, spread)), out)
-
-
-def last_body(held, dist, out, mine, spread):
-    weigh = weigh_by_distance(held, dist, spread)
+def start_body(held, counts, out, spread):
+    give_sums(weighted(held, per_client(counts[...], spread)), out)
+
+
+def again_body(held, counts, dist, out, spread):
+    give_sums(weighted(held, weigh_by_distance(counts, dist, spread)), out)
+
+
+def last_body(held, counts, dist, out, mine, spread):
+    weigh = weigh_by_distance(counts, dist, spread)
     sums = weighted(held, weigh)
     deep = out.shape[0] // HALF
     for t in range(deep):
@@ -134,7 +131,7 @@
 
 
 def distance_body(held, sums, out, rows):
-    plane, tiles = held.shape[0], held.shape[1] - 1
+    plane, tiles = held.shape[0], held.shape[1]
     whole = [functools.reduce(jnp.add, [sums[g, t] for g in range(sums.shape[0])]) for t in range(tiles // 2 + 1)]
     top = sublane() < HALF
     median = []
@@ -184,33 +181,41 @@
     updates = updates.reshape(clients, ny, rows // ny, columns)
     held = call(
         functools.partial(pack_body, tiles),
-        f32(plane, tiles + 1, SUB, LANES),
-        [HBM, HBM],
+        pltpu.HBM((plane, tiles, SUB, LANES), jnp.float32),
+        [HBM],
         "pack",
+        out_specs=HBM,
         scratch=[
             pltpu.VMEM((tiles, ny, clients * (rows // ny), LANES), jnp.float32),
-            pltpu.SMEM((clients,), jnp.int32),
+            pltpu.VMEM((tiles, plane, SUB, LANES), jnp.float32),
             pltpu.SemaphoreType.DMA((clients, tiles)),
-            pltpu.SemaphoreType.DMA,
+            pltpu.SemaphoreType.DMA((tiles,)),
         ],
-    )(*(pltpu.with_memory_space_constraint(a, pltpu.HBM) for a in (updates, sample_counts)))
+    )(pltpu.with_memory_space_constraint(updates, pltpu.HBM))
     held = lax.all_to_all(held, PLANE, 0, 0, tiled=True)
+
+    lane = jnp.arange(LANES) - lax.axis_index(PLANE) * clients
+    counts = sample_counts.astype(jnp.float32)
+    counts = jnp.where(lane == 0, counts[0], jnp.where(lane == 1, counts[1], 0.0))[None]
+    counts = counts + lax.ppermute(counts, "pair", ((0, 1), (1, 0)))
+    for axis in ("y", "x"):
+        counts = lax.psum(counts, axis)
 
     per_row = [pltpu.VMEM((plane * SUB, LANES), jnp.float32)]
     payload = f32(nfar, tiles // 2 + 1, SUB, LANES)
     along_z = functools.partial(
         lax.all_to_all, axis_name=LINE, split_axis=0, concat_axis=0, tiled=True, axis_index_groups=GROUPS
     )
-    sums = call(start_body, payload, [VMEM], "start")(held)
+    sums = call(start_body, payload, [VMEM, VMEM], "start", scratch=per_row)(held, counts)
     for iteration in range(ITERS):
         dist = call(distance_body, f32(1, LANES), [VMEM, VMEM], "distance", scratch=per_row)(held, along_z(sums))
         dist = jnp.broadcast_to(dist[None], (plane * lax.axis_size("param"), 1, LANES))
         dist = lax.all_to_all(dist, PLANE_CORES, 0, 0, tiled=True)
         if iteration < ITERS - 1:
-            sums = call(again_body, payload, [VMEM, VMEM], "again", scratch=per_row)(held, dist)
+            sums = call(again_body, payload, [VMEM] * 3, "again", scratch=per_row)(held, counts, dist)
     last, mine = call(
-        last_body, (f32(nfar * deep, LANES), f32(SUB, LANES)), [VMEM, VMEM], "last", scratch=per_row
-    )(held, dist)
+        last_body, (f32(nfar * deep, LANES), f32(SUB, LANES)), [VMEM] * 3, "last", scratch=per_row
+    )(held, counts, dist)
     median, shares = call(
         functools.partial(finish_body, clients * plane * nfar), (f32(1, columns), f32(clients)), [VMEM, VMEM], "finish"
     )(along_z(last.reshape(nfar, deep, LANES)), mine)

time: 101 us -> 118 us (1.17)
  waiting for transfers between devices: 0 us -> 19.5 us
  blocking collectives: 95.5 us -> 78.9 us
  starting transfers between devices: 0 us -> 10.5 us
  other arithmetic: 0 us -> 2.6 us
    all_to_all x1 -> x0, blocking collectives: 34.4 us -> none  [local(): held = lax.all_to_all(held, PLANE, 0, 0, tiled=True)]
    ppermute x0 -> x1, waiting for transfers between devices: none -> 19.5 us  [local(): counts = counts + lax.ppermute(counts, 'pair', ((0, 1), (1, 0)))]
    psum x0 -> x2, blocking collectives: none -> 15.8 us  [local(): counts = lax.psum(counts, axis)]
    all_to_all x0 -> x1, starting transfers between devices: none -> 9.22 us  [local(): held = lax.all_to_all(held, PLANE, 0, 0, tiled=True)]
    all_to_all x2, blocking collectives: 31.3 us -> 34.4 us  [local(): dist = lax.all_to_all(dist, PLANE_CORES, 0, 0, tiled=True)]
    ppermute x0 -> x1, starting transfers between devices: none -> 1.32 us  [local(): counts = counts + lax.ppermute(counts, 'pair', ((0, 1), (1, 0)))]
    add x0 -> x1, other arithmetic: none -> 1.3 us  [local(): counts = counts + lax.ppermute(counts, 'pair', ((0, 1), (1, 0)))]
    select_n x0 -> x1, other arithmetic: none -> 1.3 us  [local(): jnp.where(lane == 0, counts[0], jnp.where(lane == 1, counts[1], 0.0))[None]]
  transfers between devices with their start and end apart: 0 -> 2, of which waited for: 0 -> 1; matrix products, arithmetic and copies ran while one was open for 0% -> 3% of each run, Pallas kernels for 0% -> 0%
where the time goes in v4:
time: 118 us
  blocking collectives  78.9 us (67%)
  waiting for transfers between devices  19.5 us (17%)
  starting transfers between devices  10.5 us (9%)
  Pallas kernels  4.76 us (4%)
  other arithmetic  2.6 us (2%)
    all_to_all x2, blocking collectives, local(): dist = lax.all_to_all(dist, PLANE_CORES, 0, 0, tiled=True)  34.4 us
    all_to_all x2, blocking collectives, local(): along_z(sums)  20.5 us
    ppermute x1, waiting for transfers between devices, local(): counts = counts + lax.ppermute(counts, 'pair', ((0, 1), (1, 0)))  19.5 us
    psum x2, blocking collectives, local(): counts = lax.psum(counts, axis)  15.8 us
    all_to_all x1, starting transfers between devices, local(): held = lax.all_to_all(held, PLANE, 0, 0, tiled=True)  9.22 us
    all_to_all x1, blocking collectives, local(): along_z(last.reshape(nfar, deep, LANES))  8.17 us
    pallas_call x1, Pallas kernels, local(): call(functools.partial(pack_body, tiles), pltpu.HBM((plane, tiles, SUB, L...  2.7 us
  transfers between devices with their start and end apart: 2, of which 1 were waited for; matrix products, arithmetic and copies ran while one was open for 3% of the time, Pallas kernels for 0%

profile of v4, /device:TPU:1, one launch (start us, length us, event | category | flops | bytes accessed | tf_op | source)
XLA Modules:
  0.0 117.7 jit_solution(1424967235888220792)
XLA Ops:
  0.6 2.7 %pack.1 = f32[32,14,8,128]{3,2,1,0:T(8,128)} custom-call(f32[2,4,32,1792]{3,2,1,0:T(8,128)} %bitcast.9), custom_call_target="tpu_custom_call" | custom-call | tf_op jit(solution)/shard_map/pack/pallas_call | solution.py:182
  3.3 0.0 copy-start
  3.3 9.2 %all-to-all-start = ((f32[32,14,8,128]{3,2,1,0:T(8,128)}), f32[32,14,8,128]{3,2,1,0:T(8,128)S(1)}, u32[]{:S(2)}, u32[]{:S(2)}) async-start(f32[32,14,8,128]{3,2,1,0:T(8,128)} %pack.1), calls=%async_computation | async-start | bytes 3670016 | tf_op jit(solution)/shard_map/all_to_all | solution.py:195
  12.6 0.0 copy-done
  12.6 0.6 fusion
  13.2 1.3 %compare_select_fusion.1 = f32[1,128]{1,0:T(1,128)S(1)} fusion(f32[]{:T(128)} %bitcast.2, f32[]{:T(128)} %bitcast.1, s32[]{:T(128)S(6)} %mul.11), kind=kLoop, calls=%fused_computation.1 | loop fusion | flops 640 | bytes 524 | tf_op jit(solution)/shard_map/jit(_where)/select_n | solution.py:199
  14.5 1.3 %collective-permute-start = (f32[1,128]{1,0:T(1,128)S(1)}, f32[1,128]{1,0:T(1,128)S(1)}, u32[]{:S(2)}, u32[]{:S(2)}) collective-permute-start(f32[1,128]{1,0:T(1,128)S(1)} %compare_select_fusion.1), channel_id=1, source_target_pairs={{0,8},{8,0},{1,9},{9,1},{2,10},{10,2},{3,11},{11,3},{4,12},{12,4},... | collective-permute-start | bytes 1544 | tf_op jit(solution)/shard_map/ppermute | solution.py:200
  15.8 19.5 %collective-permute-done = f32[1,128]{1,0:T(1,128)S(1)} collective-permute-done((f32[1,128]{1,0:T(1,128)S(1)}, f32[1,128]{1,0:T(1,128)S(1)}, u32[]{:S(2)}, u32[]{:S(2)}) %collective-permute-start) | collective-permute-done | bytes 544 | tf_op jit(solution)/shard_map/ppermute | solution.py:200
  35.3 1.3 %fusion.1 = f32[1,128]{1,0:T(1,128)S(1)} fusion(f32[1,128]{1,0:T(1,128)S(1)} %collective-permute-done, f32[]{:T(128)} %bitcast.2, f32[]{:T(128)} %bitcast.1, s32[]{:T(128)S(6)} %mul.11), kind=kLoop, calls=%fused_computation.3 | loop fusion | flops 768 | bytes 1036 | tf_op jit(solution)/shard_map/add | solution.py:200
  36.6 7.8 %psum.14 = f32[1,128]{1,0:T(1,128)S(1)} all-reduce(f32[1,128]{1,0:T(1,128)S(1)} %fusion.1), channel_id=1, replica_groups=mesh['y'=4,'far'=4,'pair'=2,'x'=4,'param'=2] {'y'}, use_global_device_ids=true, to_apply=%region_0.1 | all-reduce | flops 128 | bytes 1024 | tf_op jit(solution)/shard_map/psum | solution.py:202
  44.5 7.9 %psum.15.counts = f32[1,128]{1,0:T(1,128)S(1)} all-reduce(f32[1,128]{1,0:T(1,128)S(1)} %psum.14), channel_id=1, replica_groups=mesh['y'=4,'far'=4,'pair'=2,'x'=4,'param'=2] {'x'}, use_global_device_ids=true, to_apply=%region_1.2 | all-reduce | flops 128 | bytes 1024 | tf_op jit(solution)/shard_map/psum | solution.py:202
  52.4 0.0 all-to-all-done.held
  52.4 0.2 start.1
  52.7 11.7 %all_to_all.30.sums = f32[4,8,8,128]{3,2,1,0:T(8,128)S(1)} all-to-all(f32[4,8,8,128]{3,2,1,0:T(8,128)S(1)} %start.1), channel_id=1, replica_groups={{0,16,40,56},{8,24,32,48},{1,17,41,57},{9,25,33,49},{2,18,42,58},{10,26..., dimensions={0} | all-to-all | bytes 262144 | tf_op jit(solution)/shard_map/all_to_all | solution.py:211
  64.4 0.3 distance.2
  64.7 19.5 %all_to_all.31.dist = f32[64,1,128]{2,1,0:T(1,128)S(1)} all-to-all(f32[64,1,128]{2,1,0:T(1,128)S(1)} %broadcast_in_dim.33), channel_id=1, replica_groups=mesh['y'=4,'far'=4,'pair'=2,'x'=4,'param'=2] {'y','pair','x','param'}, dimensions={0} | all-to-all | bytes 65536 | tf_op jit(solution)/shard_map/all_to_all | solution.py:213
  84.3 0.3 again.1
  84.5 8.8 %all_to_all.32.sums = f32[4,8,8,128]{3,2,1,0:T(8,128)S(1)} all-to-all(f32[4,8,8,128]{3,2,1,0:T(8,128)S(1)} %again.1), channel_id=1, replica_groups={{0,16,40,56},{8,24,32,48},{1,17,41,57},{9,25,33,49},{2,18,42,58},{10,26..., dimensions={0} | all-to-all | bytes 262144 | tf_op jit(solution)/shard_map/all_to_all | solution.py:211
  93.4 0.3 distance.3
  93.7 14.8 %all_to_all.33.dist = f32[64,1,128]{2,1,0:T(1,128)S(1)} all-to-all(f32[64,1,128]{2,1,0:T(1,128)S(1)} %broadcast_in_dim.35), channel_id=1, replica_groups=mesh['y'=4,'far'=4,'pair'=2,'x'=4,'param'=2] {'y','pair','x','param'}, dimensions={0} | all-to-all | bytes 65536 | tf_op jit(solution)/shard_map/all_to_all | solution.py:213
  108.6 0.3 last.1
  108.9 8.2 %all_to_all.34.got = f32[4,16,128]{2,1,0:T(8,128)S(1)} all-to-all(f32[4,16,128]{2,1,0:T(8,128)S(1)} %bitcast.6), channel_id=1, replica_groups={{0,16,40,56},{8,24,32,48},{1,17,41,57},{9,25,33,49},{2,18,42,58},{10,26..., dimensions={0} | all-to-all | bytes 65536 | tf_op jit(solution)/shard_map/all_to_all | solution.py:221
  117.0 0.6 finish.1
  (3 shorter events, 0.1 us)
Async XLA Ops:
  3.3 9.2 %copy-start = (s32[2]{0:T(128)S(1)}, s32[2]{0:T(128)}, u32[]{:S(2)}) copy-start(s32[2]{0:T(128)} %param.3) | copy-start | bytes 28
  3.3 49.1 %all-to-all-start = ((f32[32,14,8,128]{3,2,1,0:T(8,128)}), f32[32,14,8,128]{3,2,1,0:T(8,128)S(1)}, u32[]{:S(2)}, u32[]{:S(2)}) async-start(f32[32,14,8,128]{3,2,1,0:T(8,128)} %pack.1), calls=%async_computation | async-start | bytes 3670016 | tf_op jit(solution)/shard_map/all_to_all | solution.py:195
  14.5 20.8 %collective-permute-start = (f32[1,128]{1,0:T(1,128)S(1)}, f32[1,128]{1,0:T(1,128)S(1)}, u32[]{:S(2)}, u32[]{:S(2)}) collective-permute-start(f32[1,128]{1,0:T(1,128)S(1)} %compare_select_fusion.1), channel_id=1, source_target_pairs={{0,8},{8,0},{1,9},{9,1},{2,10},{10,2},{3,11},{11,3},{4,12},{12,4},... | collective-permute-start | bytes 1544 | tf_op jit(solution)/shard_map/ppermute | solution.py:200

commit v5 on v3

--- a/solution.py
+++ b/solution.py
@@ -16,6 +16,16 @@
 PLANE_CORES = ("y", "pair", "x", "param")
 LINE = ("far", "pair")
 GROUPS = ((0, 2, 5, 7), (1, 3, 4, 6))
+
+
+def place(y, pair, x):
+    return (pair + x) % 2 * 16 + (y + 4 - x) % 4 * 4 + x
+
+
+def planes():
+    order = sorted((place(y, p, x), y, p, x) for y in range(4) for p in range(2) for x in range(4))
+    return tuple(tuple(((y * 4 + f) * 2 + p) * 4 + x for _, y, p, x in order) for f in range(4))
+
 
 SUB = 8
 HALF = SUB // 2
@@ -46,33 +56,33 @@
 
 def pack_body(tiles, u_hbm, counts_hbm, out, buf, counts, sems, counts_sem):
     clients, ny, span, _ = u_hbm.shape
-    nx = span // SUB
-
-    def copy(k, j):
-        src = u_hbm.at[k, :, :, pl.ds(j * LANES, LANES)]
-        return pltpu.make_async_copy(src, buf.at[j, :, pl.ds(k * span, span), :], sems.at[k, j])
+    step = tiles * SUB
+    nx = HALF
+
+    def copy(k, y):
+        return pltpu.make_async_copy(u_hbm.at[k, y], buf.at[y, pl.ds(k * span, span), :], sems.at[k, y])
 
     fetch = pltpu.make_async_copy(counts_hbm, counts, counts_sem)
     fetch.start()
-    for j in range(tiles):
+    for y in range(ny):
         for k in range(clients):
-            copy(k, j).start()
+            copy(k, y).start()
     row = sublane()
     flip = (lax.axis_index("far") >= 2).astype(jnp.int32)
     mask = ((row >> 1) & 1) == flip
     fetch.wait()
     tile = jnp.where(row < HALF, counts[0], counts[1]).astype(jnp.float32)
-    for p in range(ny * 2 * nx):
+    for p in range(out.shape[0]):
         out[p, tiles] = tile
-    for j in range(tiles):
+    for y in range(ny):
         for k in range(clients):
-            copy(k, j).wait()
-        for y in range(ny):
-            for x in range(nx):
-                even = buf[j, y, pl.ds(x, SUB, stride=2 * nx), :]
-                odd = buf[j, y, pl.ds(nx + x, SUB, stride=2 * nx), :]
-                out[(y * 2) * nx + x, j] = jnp.where(mask, even, odd)
-                out[(y * 2 + 1) * nx + x, j] = jnp.where(mask, odd, even)
+            copy(k, y).wait()
+        for x in range(nx):
+            for t in range(tiles):
+                even = buf[y, pl.ds(t * SUB + x, SUB, stride=step), :]
+                odd = buf[y, pl.ds(t * SUB + nx + x, SUB, stride=step), :]
+                out[place(y, 0, x), t] = jnp.where(mask, even, odd)
+                out[place(y, 1, x), t] = jnp.where(mask, odd, even)
 
 
 def weighted(held, weigh):
@@ -130,7 +140,7 @@
     deep = out.shape[0] // HALF
     for t in range(deep):
         out[pl.ds(t, HALF, stride=deep), :] = sums[min(t, len(sums) - 1)][:HALF]
-    mine[...] = weigh(lax.axis_index(PLANE))
+    mine[...] = weigh(place(*(lax.axis_index(a) for a in PLANE)))
 
 
 def distance_body(held, sums, out, rows):
@@ -181,20 +191,21 @@
     tiles = columns // LANES
     deep = 2 * SUB
 
-    updates = updates.reshape(clients, ny, rows // ny, columns)
+    updates = updates.reshape(clients, rows // SUB, SUB, tiles, LANES).transpose(0, 1, 3, 2, 4)
+    updates = updates.reshape(clients, ny, rows // ny * tiles, LANES)
     held = call(
         functools.partial(pack_body, tiles),
         f32(plane, tiles + 1, SUB, LANES),
         [HBM, HBM],
         "pack",
         scratch=[
-            pltpu.VMEM((tiles, ny, clients * (rows // ny), LANES), jnp.float32),
+            pltpu.VMEM((ny, clients * (rows // ny) * tiles, LANES), jnp.float32),
             pltpu.SMEM((clients,), jnp.int32),
-            pltpu.SemaphoreType.DMA((clients, tiles)),
+            pltpu.SemaphoreType.DMA((clients, ny)),
             pltpu.SemaphoreType.DMA,
         ],
     )(*(pltpu.with_memory_space_constraint(a, pltpu.HBM) for a in (updates, sample_counts)))
-    held = lax.all_to_all(held, PLANE, 0, 0, tiled=True)
+    held = lax.all_to_all(held, CLIENT, 0, 0, tiled=True, axis_index_groups=planes())
 
     per_row = [pltpu.VMEM((plane * SUB, LANES), jnp.float32)]
     payload = f32(nfar, tiles // 2 + 1, SUB, LANES)

time: 101 us -> 100 us (0.990)
    all_to_all x2, blocking collectives: 21.6 us -> 23.8 us  [local(): along_z(sums)]
    all_to_all x2, blocking collectives: 31.3 us -> 29.9 us  [local(): dist = lax.all_to_all(dist, PLANE_CORES, 0, 0, tiled=True)]
    all_to_all x1, blocking collectives: 34.4 us -> 33.3 us  [local(): lax.all_to_all(held, CLIENT, 0, 0, tiled=True, axis_index_groups=planes())]
where the time goes in v5:
time: 100 us; the launch traced here: 99.8 us
  blocking collectives  95.2 us (95%)
  Pallas kernels  3.91 us (4%)
    all_to_all x1, blocking collectives, local(): lax.all_to_all(held, CLIENT, 0, 0, tiled=True, axis_index_groups=planes())  33.3 us
    all_to_all x2, blocking collectives, local(): dist = lax.all_to_all(dist, PLANE_CORES, 0, 0, tiled=True)  29.9 us
    all_to_all x2, blocking collectives, local(): along_z(sums)  23.8 us
    all_to_all x1, blocking collectives, local(): along_z(last.reshape(nfar, deep, LANES))  8.17 us

profile of v5, /device:TPU:1, one launch (start us, length us, event | category | flops | bytes accessed | tf_op | source)
XLA Modules:
  0.0 99.8 jit_solution(1841954616582618737)
XLA Ops:
  0.6 1.8 %pack.1 = f32[32,15,8,128]{3,2,1,0:T(8,128)S(1)} custom-call(f32[2,4,448,128]{3,2,1,0:T(8,128)} %bitcast.11, s32[2]{0:T(128)} %counts_hbm.1), custom_call_target="tpu_custom_call" | custom-call | tf_op jit(solution)/shard_map/pack/pallas_call | solution.py:196
  2.4 33.3 %all_to_all.30.held = f32[32,15,8,128]{3,2,1,0:T(8,128)S(1)} all-to-all(f32[32,15,8,128]{3,2,1,0:T(8,128)S(1)} %pack.1), channel_id=1, replica_groups={{0,74,132,206,64,138,196,14,128,202,4,78,192,10,68,142,8,66,140,198,72,..., dimensions={0} | all-to-all | bytes 3932160 | tf_op jit(solution)/shard_map/all_to_all | solution.py:208
  35.8 0.2 start.1
  35.9 14.7 %all_to_all.31.sums = f32[4,8,8,128]{3,2,1,0:T(8,128)S(1)} all-to-all(f32[4,8,8,128]{3,2,1,0:T(8,128)S(1)} %start.1), channel_id=1, replica_groups={{0,16,40,56},{8,24,32,48},{1,17,41,57},{9,25,33,49},{2,18,42,58},{10,26..., dimensions={0} | all-to-all | bytes 262144 | tf_op jit(solution)/shard_map/all_to_all | solution.py:217
  50.6 0.3 distance.2
  51.0 15.6 %all_to_all.32.dist = f32[64,1,128]{2,1,0:T(1,128)S(1)} all-to-all(f32[64,1,128]{2,1,0:T(1,128)S(1)} %broadcast_in_dim.17), channel_id=1, replica_groups=mesh['y'=4,'far'=4,'pair'=2,'x'=4,'param'=2] {'y','pair','x','param'}, dimensions={0} | all-to-all | bytes 65536 | tf_op jit(solution)/shard_map/all_to_all | solution.py:219
  66.6 0.4 again.1
  66.9 9.1 %all_to_all.33.sums = f32[4,8,8,128]{3,2,1,0:T(8,128)S(1)} all-to-all(f32[4,8,8,128]{3,2,1,0:T(8,128)S(1)} %again.1), channel_id=1, replica_groups={{0,16,40,56},{8,24,32,48},{1,17,41,57},{9,25,33,49},{2,18,42,58},{10,26..., dimensions={0} | all-to-all | bytes 262144 | tf_op jit(solution)/shard_map/all_to_all | solution.py:217
  76.0 0.3 distance.3
  76.4 14.3 %all_to_all.34.dist = f32[64,1,128]{2,1,0:T(1,128)S(1)} all-to-all(f32[64,1,128]{2,1,0:T(1,128)S(1)} %broadcast_in_dim.19), channel_id=1, replica_groups=mesh['y'=4,'far'=4,'pair'=2,'x'=4,'param'=2] {'y','pair','x','param'}, dimensions={0} | all-to-all | bytes 65536 | tf_op jit(solution)/shard_map/all_to_all | solution.py:219
  90.7 0.4 last.1
  91.1 8.2 %all_to_all.35.got = f32[4,16,128]{2,1,0:T(8,128)S(1)} all-to-all(f32[4,16,128]{2,1,0:T(8,128)S(1)} %bitcast.8), channel_id=1, replica_groups={{0,16,40,56},{8,24,32,48},{1,17,41,57},{9,25,33,49},{2,18,42,58},{10,26..., dimensions={0} | all-to-all | bytes 65536 | tf_op jit(solution)/shard_map/all_to_all | solution.py:227
  99.2 0.6 finish.1
  (2 shorter events, 0.0 us)

commit v6 on v5

--- a/solution.py
+++ b/solution.py
@@ -16,6 +16,7 @@
 PLANE_CORES = ("y", "pair", "x", "param")
 LINE = ("far", "pair")
 GROUPS = ((0, 2, 5, 7), (1, 3, 4, 6))
+FAR_FIRST = ((0, 5, 2, 7), (4, 1, 6, 3))
 
 
 def place(y, pair, x):
@@ -184,6 +185,10 @@
     shares[...] = share[0, : shares.shape[0]]
 
 
+def along_z(value, groups):
+    return lax.all_to_all(value, LINE, 0, 0, tiled=True, axis_index_groups=groups)
+
+
 def local(updates, sample_counts):
     clients, rows, columns = updates.shape
     ny, nfar, npair, nx = (lax.axis_size(a) for a in CLIENT)
@@ -209,12 +214,9 @@
 
     per_row = [pltpu.VMEM((plane * SUB, LANES), jnp.float32)]
     payload = f32(nfar, tiles // 2 + 1, SUB, LANES)
-    along_z = functools.partial(
-        lax.all_to_all, axis_name=LINE, split_axis=0, concat_axis=0, tiled=True, axis_index_groups=GROUPS
-    )
     sums = call(start_body, payload, [VMEM], "start")(held)
     for iteration in range(ITERS):
-        dist = call(distance_body, f32(1, LANES), [VMEM, VMEM], "distance", scratch=per_row)(held, along_z(sums))
+        dist = call(distance_body, f32(1, LANES), [VMEM, VMEM], "distance", scratch=per_row)(held, along_z(sums, FAR_FIRST))
         dist = jnp.broadcast_to(dist[None], (plane * lax.axis_size("param"), 1, LANES))
         dist = lax.all_to_all(dist, PLANE_CORES, 0, 0, tiled=True)
         if iteration < ITERS - 1:
@@ -224,7 +226,7 @@
     )(held, dist)
     median, shares = call(
         functools.partial(finish_body, clients * plane * nfar), (f32(1, columns), f32(clients)), [VMEM, VMEM], "finish"
-    )(along_z(last.reshape(nfar, deep, LANES)), mine)
+    )(along_z(last.reshape(nfar, deep, LANES), GROUPS), mine)
     return median, shares
 
 

time: 100 us -> 98.8 us (0.988)
  blocking collectives: 95.2 us -> 93.7 us
    all_to_all x2, blocking collectives: 29.9 us -> 28.8 us  [local(): dist = lax.all_to_all(dist, PLANE_CORES, 0, 0, tiled=True)]
where the time goes in v6:
time: 98.8 us; the launch traced here: 98.4 us
  blocking collectives  93.7 us (95%)
  Pallas kernels  3.91 us (4%)
    all_to_all x1, blocking collectives, local(): lax.all_to_all(held, CLIENT, 0, 0, tiled=True, axis_index_groups=planes())  33.3 us
    all_to_all x3, blocking collectives, along_z(): lax.all_to_all(value, LINE, 0, 0, tiled=True, axis_index_groups=groups)  31.6 us
    all_to_all x2, blocking collectives, local(): dist = lax.all_to_all(dist, PLANE_CORES, 0, 0, tiled=True)  28.8 us

profile of v6, /device:TPU:1, one launch (start us, length us, event | category | flops | bytes accessed | tf_op | source)
XLA Modules:
  0.0 98.4 jit_solution(18277135763569381077)
XLA Ops:
  0.6 1.8 %pack.1 = f32[32,15,8,128]{3,2,1,0:T(8,128)S(1)} custom-call(f32[2,4,448,128]{3,2,1,0:T(8,128)} %bitcast.11, s32[2]{0:T(128)} %counts_hbm.1), custom_call_target="tpu_custom_call" | custom-call | tf_op jit(solution)/shard_map/pack/pallas_call | solution.py:201
  2.4 33.3 %all_to_all.30.held = f32[32,15,8,128]{3,2,1,0:T(8,128)S(1)} all-to-all(f32[32,15,8,128]{3,2,1,0:T(8,128)S(1)} %pack.1), channel_id=1, replica_groups={{0,74,132,206,64,138,196,14,128,202,4,78,192,10,68,142,8,66,140,198,72,..., dimensions={0} | all-to-all | bytes 3932160 | tf_op jit(solution)/shard_map/all_to_all | solution.py:213
  35.8 0.2 start.1
  35.9 14.4 %all_to_all.31.sums = f32[4,8,8,128]{3,2,1,0:T(8,128)S(1)} all-to-all(f32[4,8,8,128]{3,2,1,0:T(8,128)S(1)} %start.1), channel_id=1, replica_groups={{0,40,16,56},{32,8,48,24},{1,41,17,57},{33,9,49,25},{2,42,18,58},{34,10..., dimensions={0} | all-to-all | bytes 262144 | tf_op jit(solution)/shard_map/all_to_all | solution.py:189
  50.3 0.3 distance.2
  50.6 14.9 %all_to_all.32.dist = f32[64,1,128]{2,1,0:T(1,128)S(1)} all-to-all(f32[64,1,128]{2,1,0:T(1,128)S(1)} %broadcast_in_dim.17), channel_id=1, replica_groups=mesh['y'=4,'far'=4,'pair'=2,'x'=4,'param'=2] {'y','pair','x','param'}, dimensions={0} | all-to-all | bytes 65536 | tf_op jit(solution)/shard_map/all_to_all | solution.py:221
  65.5 0.4 again.1
  65.9 8.7 %all_to_all.33.sums = f32[4,8,8,128]{3,2,1,0:T(8,128)S(1)} all-to-all(f32[4,8,8,128]{3,2,1,0:T(8,128)S(1)} %again.1), channel_id=1, replica_groups={{0,40,16,56},{32,8,48,24},{1,41,17,57},{33,9,49,25},{2,42,18,58},{34,10..., dimensions={0} | all-to-all | bytes 262144 | tf_op jit(solution)/shard_map/all_to_all | solution.py:189
  74.5 0.3 distance.3
  74.9 13.9 %all_to_all.34.dist = f32[64,1,128]{2,1,0:T(1,128)S(1)} all-to-all(f32[64,1,128]{2,1,0:T(1,128)S(1)} %broadcast_in_dim.19), channel_id=1, replica_groups=mesh['y'=4,'far'=4,'pair'=2,'x'=4,'param'=2] {'y','pair','x','param'}, dimensions={0} | all-to-all | bytes 65536 | tf_op jit(solution)/shard_map/all_to_all | solution.py:221
  88.8 0.4 last.1
  89.2 8.6 %all_to_all.35.got = f32[4,16,128]{2,1,0:T(8,128)S(1)} all-to-all(f32[4,16,128]{2,1,0:T(8,128)S(1)} %bitcast.8), channel_id=1, replica_groups={{0,16,40,56},{8,24,32,48},{1,17,41,57},{9,25,33,49},{2,18,42,58},{10,26..., dimensions={0} | all-to-all | bytes 65536 | tf_op jit(solution)/shard_map/all_to_all | solution.py:189
  97.8 0.6 finish.1
  (2 shorter events, 0.0 us)

commit v7 on v5

--- a/solution.py
+++ b/solution.py
@@ -15,7 +15,7 @@
 PLANE = ("y", "pair", "x")
 PLANE_CORES = ("y", "pair", "x", "param")
 LINE = ("far", "pair")
-GROUPS = ((0, 2, 5, 7), (1, 3, 4, 6))
+FAR_FIRST = ((0, 5, 2, 7), (4, 1, 6, 3))
 
 
 def place(y, pair, x):
@@ -138,8 +138,12 @@
     weigh = weigh_by_distance(held, dist, spread)
     sums = weighted(held, weigh)
     deep = out.shape[0] // HALF
+    odd = (lax.axis_index("pair") + lax.axis_index("far") // 2) % 2 == 1
     for t in range(deep):
-        out[pl.ds(t, HALF, stride=deep), :] = sums[min(t, len(sums) - 1)][:HALF]
+        rows = sums[min(t, len(sums) - 1)]
+        for g in range(HALF):
+            one, other = (z // 2 for z in (FAR_FIRST[0][g], FAR_FIRST[1][g]))
+            out[pl.ds(g * deep + t, 1), :] = jnp.where(odd, rows[other : other + 1], rows[one : one + 1])
     mine[...] = weigh(place(*(lax.axis_index(a) for a in PLANE)))
 
 
@@ -182,6 +186,10 @@
     lane = lax.broadcasted_iota(jnp.int32, (1, LANES), 1)
     share = jnp.where(lane == 0, share[:1], share[HALF : HALF + 1])
     shares[...] = share[0, : shares.shape[0]]
+
+
+def along_z(value):
+    return lax.all_to_all(value, LINE, 0, 0, tiled=True, axis_index_groups=FAR_FIRST)
 
 
 def local(updates, sample_counts):
@@ -209,9 +217,6 @@
 
     per_row = [pltpu.VMEM((plane * SUB, LANES), jnp.float32)]
     payload = f32(nfar, tiles // 2 + 1, SUB, LANES)
-    along_z = functools.partial(
-        lax.all_to_all, axis_name=LINE, split_axis=0, concat_axis=0, tiled=True, axis_index_groups=GROUPS
-    )
     sums = call(start_body, payload, [VMEM], "start")(held)
     for iteration in range(ITERS):
         dist = call(distance_body, f32(1, LANES), [VMEM, VMEM], "distance", scratch=per_row)(held, along_z(sums))

time: 100 us -> 98.6 us (0.986)
  blocking collectives: 95.2 us -> 93.7 us
    all_to_all x2, blocking collectives: 29.9 us -> 28.8 us  [local(): dist = lax.all_to_all(dist, PLANE_CORES, 0, 0, tiled=True)]
where the time goes in v7:
time: 98.6 us; the launch traced here: 98.3 us
  blocking collectives  93.7 us (95%)
  Pallas kernels  3.92 us (4%)
    all_to_all x1, blocking collectives, local(): lax.all_to_all(held, CLIENT, 0, 0, tiled=True, axis_index_groups=planes())  33.3 us
    all_to_all x3, blocking collectives, along_z(): lax.all_to_all(value, LINE, 0, 0, tiled=True, axis_index_groups=FAR_FIRST)  31.5 us
    all_to_all x2, blocking collectives, local(): dist = lax.all_to_all(dist, PLANE_CORES, 0, 0, tiled=True)  28.8 us

profile of v7, /device:TPU:1, one launch (start us, length us, event | category | flops | bytes accessed | tf_op | source)
XLA Modules:
  0.0 98.3 jit_solution(4862422589126528330)
XLA Ops:
  0.6 1.8 %pack.1 = f32[32,15,8,128]{3,2,1,0:T(8,128)S(1)} custom-call(f32[2,4,448,128]{3,2,1,0:T(8,128)} %bitcast.11, s32[2]{0:T(128)} %counts_hbm.1), custom_call_target="tpu_custom_call" | custom-call | tf_op jit(solution)/shard_map/pack/pallas_call | solution.py:204
  2.4 33.3 %all_to_all.30.held = f32[32,15,8,128]{3,2,1,0:T(8,128)S(1)} all-to-all(f32[32,15,8,128]{3,2,1,0:T(8,128)S(1)} %pack.1), channel_id=1, replica_groups={{0,74,132,206,64,138,196,14,128,202,4,78,192,10,68,142,8,66,140,198,72,..., dimensions={0} | all-to-all | bytes 3932160 | tf_op jit(solution)/shard_map/all_to_all | solution.py:216
  35.8 0.2 start.1
  35.9 14.4 %all_to_all.31.sums = f32[4,8,8,128]{3,2,1,0:T(8,128)S(1)} all-to-all(f32[4,8,8,128]{3,2,1,0:T(8,128)S(1)} %start.1), channel_id=1, replica_groups={{0,40,16,56},{32,8,48,24},{1,41,17,57},{33,9,49,25},{2,42,18,58},{34,10..., dimensions={0} | all-to-all | bytes 262144 | tf_op jit(solution)/shard_map/all_to_all | solution.py:192
  50.3 0.3 distance.2
  50.6 14.9 %all_to_all.32.dist = f32[64,1,128]{2,1,0:T(1,128)S(1)} all-to-all(f32[64,1,128]{2,1,0:T(1,128)S(1)} %broadcast_in_dim.17), channel_id=1, replica_groups=mesh['y'=4,'far'=4,'pair'=2,'x'=4,'param'=2] {'y','pair','x','param'}, dimensions={0} | all-to-all | bytes 65536 | tf_op jit(solution)/shard_map/all_to_all | solution.py:224
  65.5 0.4 again.1
  65.9 8.7 %all_to_all.33.sums = f32[4,8,8,128]{3,2,1,0:T(8,128)S(1)} all-to-all(f32[4,8,8,128]{3,2,1,0:T(8,128)S(1)} %again.1), channel_id=1, replica_groups={{0,40,16,56},{32,8,48,24},{1,41,17,57},{33,9,49,25},{2,42,18,58},{34,10..., dimensions={0} | all-to-all | bytes 262144 | tf_op jit(solution)/shard_map/all_to_all | solution.py:192
  74.5 0.3 distance.3
  74.9 13.9 %all_to_all.34.dist = f32[64,1,128]{2,1,0:T(1,128)S(1)} all-to-all(f32[64,1,128]{2,1,0:T(1,128)S(1)} %broadcast_in_dim.19), channel_id=1, replica_groups=mesh['y'=4,'far'=4,'pair'=2,'x'=4,'param'=2] {'y','pair','x','param'}, dimensions={0} | all-to-all | bytes 65536 | tf_op jit(solution)/shard_map/all_to_all | solution.py:224
  88.8 0.4 last.1
  89.2 8.5 %all_to_all.35.got = f32[4,16,128]{2,1,0:T(8,128)S(1)} all-to-all(f32[4,16,128]{2,1,0:T(8,128)S(1)} %bitcast.8), channel_id=1, replica_groups={{0,40,16,56},{32,8,48,24},{1,41,17,57},{33,9,49,25},{2,42,18,58},{34,10..., dimensions={0} | all-to-all | bytes 65536 | tf_op jit(solution)/shard_map/all_to_all | solution.py:192
  97.7 0.6 finish.1
  (2 shorter events, 0.0 us)

commit v8 on v7

--- a/solution.py
+++ b/solution.py
@@ -94,7 +94,7 @@
         return (*sums, accs[tiles] + w)
 
     zero = jnp.zeros((SUB, LANES), jnp.float32)
-    accs = lax.fori_loop(0, plane, step, (zero,) * (tiles + 1), unroll=8)
+    accs = lax.fori_loop(0, plane, step, (zero,) * (tiles + 1), unroll=plane)
     return [a + pltpu.roll(a, HALF, 0) for a in accs]
 
 
@@ -165,7 +165,7 @@
         rows[pl.ds(pl.multiple_of(src * SUB, SUB), SUB), :] = acc
         return carry
 
-    lax.fori_loop(0, plane, step, 0, unroll=8)
+    lax.fori_loop(0, plane, step, 0, unroll=plane)
     clients = 2 * plane
     lanes = []
     for g in range(clients // SUB):

time: 98.6 us -> 98.4 us (level)
  no operation moved by 1% of the time
where the time goes in v8:
time: 98.4 us; the launch traced here: 98.1 us
  blocking collectives  93.7 us (95%)
  Pallas kernels  3.74 us (4%)
    all_to_all x1, blocking collectives, local(): lax.all_to_all(held, CLIENT, 0, 0, tiled=True, axis_index_groups=planes())  33.3 us
    all_to_all x3, blocking collectives, along_z(): lax.all_to_all(value, LINE, 0, 0, tiled=True, axis_index_groups=FAR_FIRST)  31.5 us
    all_to_all x2, blocking collectives, local(): dist = lax.all_to_all(dist, PLANE_CORES, 0, 0, tiled=True)  28.8 us

profile of v8, /device:TPU:1, one launch (start us, length us, event | category | flops | bytes accessed | tf_op | source)
XLA Modules:
  0.0 98.1 jit_solution(14117388285973989491)
XLA Ops:
  0.6 1.8 %pack.1 = f32[32,15,8,128]{3,2,1,0:T(8,128)S(1)} custom-call(f32[2,4,448,128]{3,2,1,0:T(8,128)} %bitcast.11, s32[2]{0:T(128)} %counts_hbm.1), custom_call_target="tpu_custom_call" | custom-call | tf_op jit(solution)/shard_map/pack/pallas_call | solution.py:204
  2.4 33.3 %all_to_all.30.held = f32[32,15,8,128]{3,2,1,0:T(8,128)S(1)} all-to-all(f32[32,15,8,128]{3,2,1,0:T(8,128)S(1)} %pack.1), channel_id=1, replica_groups={{0,74,132,206,64,138,196,14,128,202,4,78,192,10,68,142,8,66,140,198,72,..., dimensions={0} | all-to-all | bytes 3932160 | tf_op jit(solution)/shard_map/all_to_all | solution.py:216
  35.8 0.2 start.1
  35.9 14.4 %all_to_all.31.sums = f32[4,8,8,128]{3,2,1,0:T(8,128)S(1)} all-to-all(f32[4,8,8,128]{3,2,1,0:T(8,128)S(1)} %start.1), channel_id=1, replica_groups={{0,40,16,56},{32,8,48,24},{1,41,17,57},{33,9,49,25},{2,42,18,58},{34,10..., dimensions={0} | all-to-all | bytes 262144 | tf_op jit(solution)/shard_map/all_to_all | solution.py:192
  50.3 0.3 distance.2
  50.6 14.9 %all_to_all.32.dist = f32[64,1,128]{2,1,0:T(1,128)S(1)} all-to-all(f32[64,1,128]{2,1,0:T(1,128)S(1)} %broadcast_in_dim.17), channel_id=1, replica_groups=mesh['y'=4,'far'=4,'pair'=2,'x'=4,'param'=2] {'y','pair','x','param'}, dimensions={0} | all-to-all | bytes 65536 | tf_op jit(solution)/shard_map/all_to_all | solution.py:224
  65.5 0.3 again.1
  65.8 8.7 %all_to_all.33.sums = f32[4,8,8,128]{3,2,1,0:T(8,128)S(1)} all-to-all(f32[4,8,8,128]{3,2,1,0:T(8,128)S(1)} %again.1), channel_id=1, replica_groups={{0,40,16,56},{32,8,48,24},{1,41,17,57},{33,9,49,25},{2,42,18,58},{34,10..., dimensions={0} | all-to-all | bytes 262144 | tf_op jit(solution)/shard_map/all_to_all | solution.py:192
  74.4 0.3 distance.3
  74.8 13.9 %all_to_all.34.dist = f32[64,1,128]{2,1,0:T(1,128)S(1)} all-to-all(f32[64,1,128]{2,1,0:T(1,128)S(1)} %broadcast_in_dim.19), channel_id=1, replica_groups=mesh['y'=4,'far'=4,'pair'=2,'x'=4,'param'=2] {'y','pair','x','param'}, dimensions={0} | all-to-all | bytes 65536 | tf_op jit(solution)/shard_map/all_to_all | solution.py:224
  88.7 0.3 last.1
  89.0 8.5 %all_to_all.35.got = f32[4,16,128]{2,1,0:T(8,128)S(1)} all-to-all(f32[4,16,128]{2,1,0:T(8,128)S(1)} %bitcast.8), channel_id=1, replica_groups={{0,40,16,56},{32,8,48,24},{1,41,17,57},{33,9,49,25},{2,42,18,58},{34,10..., dimensions={0} | all-to-all | bytes 65536 | tf_op jit(solution)/shard_map/all_to_all | solution.py:192
  97.5 0.6 finish.1
  (2 shorter events, 0.0 us)
